TPU v7x, 512 devices: a whole 4x8x8 slice. The times are simulated.
512 devices in a mesh: depth: 32 (over z, x), rows: 16 (over y, core).
Axes of the slice: x: 4, y: 8, z: 8, core: 2. Of those that a mesh axis runs over, the one named last changes fastest.
Arguments:
- spectrum: bfloat16 [2, 4096, 4096], P(None, 'rows'), may hold values from -6 to 6
- plane_index: int32 [32], P('depth'), may hold values from 0 to 2047
- kernel_width: int32 [32], P('depth'), may hold values from 1 to 3
- focus_gain: float32 [32], P('depth'), may hold values from 0.5 to 30
Outputs:
- depth_map: float32 [256, 4096], P('rows', 'depth')
- focused: float32 [2, 256, 4096], P(None, 'rows', 'depth')
All inputs are finite; a program needn't handle non-finite values.
Results may differ from a plain program's by a relative error of at most 0.0003.
Values may be sent and summed in bfloat16 or wider, within the bound.
No kernel may reach another device: no remote copies, remote signals or barrier semaphores. Data moves between devices by JAX's collectives and lax.ppermute only.
A program may use at most 192 MiB of HBM per device.

v0:
```python
from functools import partial
import math

import jax
import jax.numpy as jnp
from jax import lax
from jax.sharding import PartitionSpec as P

NX = 4096
RADIX = 64
Y_WIN = 256
DEPTHS = 2048
MAXWIDTH = 3


def with_halo(block, sides, width):
    for axis, dim in sides:
        count = lax.axis_size(axis)
        forward = [(i, i + 1) for i in range(count - 1)]
        backward = [(target, source) for source, target in forward]
        low = lax.ppermute(
            lax.slice_in_dim(block, block.shape[dim] - width, None, axis=dim), axis, forward
        )
        high = lax.ppermute(lax.slice_in_dim(block, 0, width, axis=dim), axis, backward)
        block = jnp.concatenate([low, block, high], axis=dim)
    return block


def combined_all(value, axis, join):
    pieces = jax.tree.map(lambda part: lax.all_gather(part, axis), value)
    head = jax.tree.map(lambda part: part[0], pieces)
    tail = jax.tree.map(lambda part: part[1:], pieces)
    so_far, _ = lax.scan(lambda so_far, piece: (join(so_far, piece), None), head, tail)
    return so_far


def line_phase(plane_index, freqs):
    signed = jnp.where(freqs < NX // 2, freqs, freqs - NX)
    square = signed * signed
    upper_part = (square // NX)[None, :]
    lower_part = (square % NX)[None, :]
    depth_col = plane_index[:, None]
    turns = (depth_col * lower_part + NX * (depth_col * upper_part % NX)) % (NX * NX)
    return turns.astype(jnp.float32) * (-2.0 * math.pi / (NX * NX))


def sobel_energy(padded):
    vertical = padded[..., :-2, :] + 2.0 * padded[..., 1:-1, :] + padded[..., 2:, :]
    across = vertical[..., :, 2:] - vertical[..., :, :-2]
    horizontal = padded[..., :, :-2] + 2.0 * padded[..., :, 1:-1] + padded[..., :, 2:]
    downward = horizontal[..., 2:, :] - horizontal[..., :-2, :]
    return across * across + downward * downward


def smooth_columns(energy, radius):
    extent = energy.shape[-1]
    padded = jnp.pad(energy, [(0, 0)] * (energy.ndim - 1) + [(MAXWIDTH, MAXWIDTH)])
    summed = jnp.zeros_like(energy)
    for offset in range(-MAXWIDTH, MAXWIDTH + 1):
        inside = (abs(offset) <= radius).astype(jnp.float32)
        summed = summed + inside * padded[..., MAXWIDTH + offset : MAXWIDTH + offset + extent]
    return summed / (2 * radius + 1).astype(jnp.float32)


def section_tables(out_blocks):
    counter = jnp.arange(RADIX, dtype=jnp.int32)
    first_turns = counter[:, None] * counter[None, :] % RADIX
    first_angle = first_turns.astype(jnp.float32) * (2.0 * math.pi / RADIX)
    twist_angle = (counter[:, None] * counter[None, :]).astype(jnp.float32) * (2.0 * math.pi / NX)
    kept_index = jnp.arange(out_blocks, dtype=jnp.int32)
    second_turns = counter[:, None] * kept_index[None, :] % RADIX
    second_angle = second_turns.astype(jnp.float32) * (2.0 * math.pi / RADIX)
    return (
        jnp.cos(first_angle),
        jnp.sin(first_angle),
        jnp.cos(twist_angle),
        jnp.sin(twist_angle),
        jnp.cos(second_angle),
        jnp.sin(second_angle),
    )


def complex_einsum(form, real_part, imag_part, table_real, table_imag):
    product = partial(jnp.einsum, form, precision=lax.Precision.HIGHEST)
    return (
        product(real_part, table_real) - product(imag_part, table_imag),
        product(real_part, table_imag) + product(imag_part, table_real),
    )


def transform_last(real_part, imag_part, out_blocks):
    leading = real_part.shape[:-1]
    tables = section_tables(out_blocks)
    shaped_real = real_part.reshape(leading + (RADIX, RADIX))
    shaped_imag = imag_part.reshape(leading + (RADIX, RADIX))
    section_real, section_imag = complex_einsum(
        "...dc,da->...ca", shaped_real, shaped_imag, tables[0], tables[1]
    )
    twisted_real = section_real * tables[2] - section_imag * tables[3]
    twisted_imag = section_real * tables[3] + section_imag * tables[2]
    final_real, final_imag = complex_einsum(
        "...ca,cb->...ba", twisted_real, twisted_imag, tables[4], tables[5]
    )
    new_shape = leading + (out_blocks * RADIX,)
    return (final_real.reshape(new_shape) / RADIX, final_imag.reshape(new_shape) / RADIX)


def transform_middle(real_part, imag_part, out_blocks):
    leading = real_part.shape[:-2]
    columns_n = real_part.shape[-1]
    tables = section_tables(out_blocks)
    shaped_real = real_part.reshape(leading + (RADIX, RADIX, columns_n))
    shaped_imag = imag_part.reshape(leading + (RADIX, RADIX, columns_n))
    section_real, section_imag = complex_einsum(
        "...dcw,da->...caw", shaped_real, shaped_imag, tables[0], tables[1]
    )
    twist_real = tables[2][:, :, None]
    twist_imag = tables[3][:, :, None]
    twisted_real = section_real * twist_real - section_imag * twist_imag
    twisted_imag = section_real * twist_imag + section_imag * twist_real
    final_real, final_imag = complex_einsum(
        "...caw,cb->...baw", twisted_real, twisted_imag, tables[4], tables[5]
    )
    new_shape = leading + (out_blocks * RADIX, columns_n)
    return (final_real.reshape(new_shape) / RADIX, final_imag.reshape(new_shape) / RADIX)


def rotate(spectra, plane_index, rows_freq, cols_freq):
    row_phase = line_phase(plane_index, rows_freq)
    col_phase = line_phase(plane_index, cols_freq)
    row_cos = jnp.cos(row_phase)[:, :, None]
    row_sin = jnp.sin(row_phase)[:, :, None]
    col_cos = jnp.cos(col_phase)[:, None, :]
    col_sin = jnp.sin(col_phase)[:, None, :]
    factor_real = row_cos * col_cos - row_sin * col_sin
    factor_imag = row_cos * col_sin + row_sin * col_cos
    real_in = spectra[0].astype(jnp.float32)
    imag_in = spectra[1].astype(jnp.float32)
    return (
        real_in * factor_real - imag_in * factor_imag,
        real_in * factor_imag + imag_in * factor_real,
    )


def combine(first_records, second_records):
    peak = jnp.maximum(first_records[0], second_records[0])
    former = jnp.exp(first_records[0] - peak)
    latest = jnp.exp(second_records[0] - peak)
    return (
        peak,
        first_records[1] * former + second_records[1] * latest,
        first_records[2] * former + second_records[2] * latest,
        first_records[3] * former + second_records[3] * latest,
        first_records[4] * former + second_records[4] * latest,
    )


def shards(spectrum, plane_index, kernel_width, focus_gain):
    row_place = lax.axis_index("rows")
    swapped = lax.all_to_all(spectrum, "rows", split_axis=2, concat_axis=1, tiled=True)
    band_cols = swapped.shape[2]
    rows_freq = jnp.arange(NX, dtype=jnp.int32)
    cols_freq = row_place * band_cols + jnp.arange(band_cols, dtype=jnp.int32)
    real_rot, imag_rot = rotate(swapped, plane_index, rows_freq, cols_freq)
    real_mid, imag_mid = transform_middle(real_rot, imag_rot, Y_WIN // RADIX)
    pieces = (
        lax.all_to_all(real_mid, "rows", split_axis=1, concat_axis=2, tiled=True),
        lax.all_to_all(imag_mid, "rows", split_axis=1, concat_axis=2, tiled=True),
    )
    real_part, imag_part = transform_last(pieces[0], pieces[1], RADIX)
    intensity = real_part * real_part + imag_part * imag_part
    rimmed = with_halo(intensity, (("rows", 1),), 1)
    padded = jnp.pad(rimmed, ((0, 0), (0, 0), (1, 1)))
    energy = sobel_energy(padded)
    smoothed = smooth_columns(energy, kernel_width[:, None, None])
    scores = focus_gain[:, None, None] * jnp.log(1.0 + smoothed)
    highest = jnp.max(scores, axis=0)
    weights = jnp.exp(scores - highest[None])
    depth_value = (plane_index.astype(jnp.float32) / DEPTHS)[:, None, None]
    summed = jnp.sum(weights, axis=0)
    depth_sum = jnp.sum(weights * depth_value, axis=0)
    real_sum = jnp.sum(weights * real_part, axis=0)
    imag_sum = jnp.sum(weights * imag_part, axis=0)
    merged = combined_all((highest, summed, depth_sum, real_sum, imag_sum), "depth", combine)
    columns_dev = NX // lax.axis_size("depth")
    start_col = lax.axis_index("depth") * columns_dev
    pieces = tuple(
        (lax.dynamic_slice_in_dim(record, start_col, columns_dev, 1) for record in merged)
    )
    total_weight = pieces[1]
    total_depth = pieces[2]
    total_real = pieces[3]
    total_imag = pieces[4]
    depth_map = total_depth / total_weight
    focused = jnp.stack([total_real / total_weight, total_imag / total_weight])
    return (depth_map, focused)


def solution(mesh):
    return jax.shard_map(
        shards,
        mesh=mesh,
        in_specs=(P(None, "rows", None), P("depth"), P("depth"), P("depth")),
        out_specs=(P("rows", "depth"), P(None, "rows", "depth")),
        check_vma=False,
    )
```

profile of v0, /device:TPU:1, one launch (start us, length us, event | category | flops | bytes accessed | tf_op | source)
XLA Modules:
  0.0 851.2 jit_solution(15717054327686003434)
XLA Ops:
  7.2 11.1 %copy.73 = bf16[2,256,4096]{1,0,2:T(2,128)(2,1)} copy(bf16[2,256,4096]{2,1,0:T(8,128)(2,1)} %param.6) | data formatting | bytes 8388608 | tf_op args[0]
  18.3 11.1 %all-to-all-start = ((bf16[2,256,4096]{1,0,2:T(2,128)(2,1)}), bf16[2,256,4096]{1,0,2:T(2,128)(2,1)}, u32[]{:S(2)}, u32[]{:S(2)}) async-start(bf16[2,256,4096]{1,0,2:T(2,128)(2,1)} %copy.73), calls=%async_computation | async-start | bytes 8388608 | tf_op jit(solution)/shard_map/all_to_all | solution.py:160
  32.2 90.7 %all-to-all-done = bf16[2,256,4096]{1,0,2:T(2,128)(2,1)} async-done(((bf16[2,256,4096]{1,0,2:T(2,128)(2,1)}), bf16[2,256,4096]{1,0,2:T(2,128)(2,1)}, u32[]{:S(2)}, u32[]{:S(2)}) %all-to-all-start) | async-done | bytes 4194336 | tf_op jit(solution)/shard_map/all_to_all | solution.py:160
  123.0 2.7 copy.74
  125.7 4.3 slice_convert_fusion.1
  130.0 5.4 copy.75
  135.4 5.4 copy.78
  140.8 5.1 multiply_subtract_fusion
  146.0 6.3 fusion.17
  152.3 6.3 fusion.19
  158.6 6.7 fusion.25
  165.3 8.2 fusion.6
  173.5 4.4 fusion.11
  177.9 4.4 fusion.36
  183.3 5.8 all-to-all-start.1
  189.1 6.6 fusion.9
  195.7 4.4 fusion.42
  201.1 7.2 all-to-all-start.2
  210.9 9.0 %all-to-all-done.2 = f32[1,256,256]{2,0,1:T(1,128)S(1)} async-done(((f32[1,256,256]{2,0,1:T(1,128)}), f32[1,256,256]{2,0,1:T(1,128)S(1)}, u32[]{:S(2)}, u32[]{:S(2)}) %all-to-all-start.2) | async-done | bytes 262176 | tf_op jit(solution)/shard_map/all_to_all | solution.py:168
  227.6 2.4 collective-permute-start.1
  230.3 2.4 collective-permute-done.1
  238.6 98.5 %all-gather.6.cloned.1.call-done = f32[32,16,4096]{2,1,0:T(8,128)} async-done(((f32[1,16,4096]{2,1,0:T(8,128)}), f32[32,16,4096]{2,1,0:T(8,128)}) %all-gather.6.cloned.1.call-update) | async-done | bytes 8388624 | tf_op jit(solution)/shard_map/all_gather | solution.py:30
  337.1 7.4 slice.133
  344.5 96.4 %all-gather.14.cloned.1.call-done = f32[32,16,4096]{2,1,0:T(8,128)} async-done(((f32[1,16,4096]{2,1,0:T(8,128)}), f32[32,16,4096]{2,1,0:T(8,128)}) %all-gather.14.cloned.1.call-update) | async-done | bytes 8388624 | tf_op jit(solution)/shard_map/all_gather | solution.py:30
  440.9 7.4 slice.137
  448.3 96.5 %all-gather.8.cloned.1.call-done = f32[32,16,4096]{2,1,0:T(8,128)} async-done(((f32[1,16,4096]{2,1,0:T(8,128)}), f32[32,16,4096]{2,1,0:T(8,128)}) %all-gather.8.cloned.1.call-update) | async-done | bytes 8388624 | tf_op jit(solution)/shard_map/all_gather | solution.py:30
  544.8 7.4 slice.134
  552.2 96.3 %all-gather.10.cloned.1.call-done = f32[32,16,4096]{2,1,0:T(8,128)} async-done(((f32[1,16,4096]{2,1,0:T(8,128)}), f32[32,16,4096]{2,1,0:T(8,128)}) %all-gather.10.cloned.1.call-update) | async-done | bytes 8388624 | tf_op jit(solution)/shard_map/all_gather | solution.py:30
  648.5 7.4 slice.135
  659.8 92.4 %all-gather.12.cloned.1.call-done = f32[32,16,4096]{2,1,0:T(8,128)} async-done(((f32[1,16,4096]{2,1,0:T(8,128)}), f32[32,16,4096]{2,1,0:T(8,128)}) %all-gather.12.cloned.1.call-update) | async-done | bytes 8388624 | tf_op jit(solution)/shard_map/all_gather | solution.py:30
  753.2 7.4 slice.136
  760.6 82.4 %while.18 = (s32[]{:T(128)}, f32[16,4096]{1,0:T(8,128)S(1)}, f32[16,4096]{1,0:T(8,128)S(1)}, f32[16,4096]{1,0:T(8,128)S(1)}, f32[16,4096]{1,0:T(8,128)S(1)}, /*i...) while((s32[]{:T(128)}, f32[16,4096]{1,0:T(8,128)S(1)}, ...), condition=%wide.region_1.2_spmd, body=%wide.region_0.1_spmd.sunk | while | flops 983042 | bytes 4980869 | solution.py:33
  (124 shorter events, 107.2 us)
Async XLA Ops:
  18.3 104.7 %all-to-all-start = ((bf16[2,256,4096]{1,0,2:T(2,128)(2,1)}), bf16[2,256,4096]{1,0,2:T(2,128)(2,1)}, u32[]{:S(2)}, u32[]{:S(2)}) async-start(bf16[2,256,4096]{1,0,2:T(2,128)(2,1)} %copy.73), calls=%async_computation | async-start | bytes 8388608 | tf_op jit(solution)/shard_map/all_to_all | solution.py:160
  173.5 8.7 %copy-start = (f32[64,64,256]{2,1,0:T(8,128)}, f32[64,64,256]{2,1,0:T(8,128)S(1)}, u32[]{:S(2)}) copy-start(f32[64,64,256]{2,1,0:T(8,128)S(1)} %get-tuple-element.99) | copy-start | bytes 12582916
  173.5 8.7 %copy-start.2 = (f32[64,64,256]{2,1,0:T(8,128)}, f32[64,64,256]{2,1,0:T(8,128)S(1)}, u32[]{:S(2)}) copy-start(f32[64,64,256]{2,1,0:T(8,128)S(1)} %get-tuple-element.100) | copy-start | bytes 12582916
  183.3 17.8 %all-to-all-start.1 = ((f32[1,256,256]{2,0,1:T(1,128)}), f32[1,256,256]{2,0,1:T(1,128)S(1)}, u32[]{:S(2)}, u32[]{:S(2)}) async-start(f32[1,256,256]{2,0,1:T(1,128)} %copy.88), calls=%async_computation.1 | async-start | bytes 524288 | tf_op jit(solution)/shard_map/all_to_all | solution.py:167
  189.1 6.6 copy-start.1
  201.1 18.8 %all-to-all-start.2 = ((f32[1,256,256]{2,0,1:T(1,128)}), f32[1,256,256]{2,0,1:T(1,128)S(1)}, u32[]{:S(2)}, u32[]{:S(2)}) async-start(f32[1,256,256]{2,0,1:T(1,128)} %copy.95), calls=%async_computation.2 | async-start | bytes 524288 | tf_op jit(solution)/shard_map/all_to_all | solution.py:168
  208.3 128.8 %all-gather.6.cloned.1.call-start = ((), (), s32[]{:S(2)}) async-start(), calls=%async_computation.3 | async-start | bytes 8650752 | tf_op jit(solution)/shard_map/all_gather | solution.py:30
  225.7 4.6 collective-permute-start
  227.6 5.1 collective-permute-start.1
  234.7 206.2 %all-gather.14.cloned.1.call-start = ((), (), s32[]{:S(2)}) async-start(), calls=%async_computation.7 | async-start | bytes 8650752 | tf_op jit(solution)/shard_map/all_gather | solution.py:30
  235.5 309.3 %all-gather.8.cloned.1.call-start = ((), (), s32[]{:S(2)}) async-start(), calls=%async_computation.4 | async-start | bytes 8650752 | tf_op jit(solution)/shard_map/all_gather | solution.py:30
  237.5 411.0 %all-gather.10.cloned.1.call-start = ((), (), s32[]{:S(2)}) async-start(), calls=%async_computation.5 | async-start | bytes 8650752 | tf_op jit(solution)/shard_map/all_gather | solution.py:30
  238.0 514.1 %all-gather.12.cloned.1.call-start = ((), (), s32[]{:S(2)}) async-start(), calls=%async_computation.6 | async-start | bytes 8650752 | tf_op jit(solution)/shard_map/all_gather | solution.py:30
Sparse Core Ops, SparseCore 0:
  234.9 102.1 all-gather.5
  340.3 100.6 all-gather.13
  444.1 100.6 all-gather.7
  547.8 100.6 all-gather.9
  651.5 100.6 all-gather.11
where the time goes:
time: 857 us; the launch traced here: 851 us
  waiting for transfers between devices  584 us (68%)
  other arithmetic  97.1 us (11%)
  local copies, waits for them, and re-layouts  70.1 us (8%)
  matrix products  54.1 us (6%)
  starting transfers between devices  29.2 us (3%)
  between operations  16.6 us (2%)
    all_gather x5, waiting for transfers between devices, combined_all(): pieces = jax.tree.map(lambda part: lax.all_gather(part, axis), value)  480 us
    all_to_all x1, waiting for transfers between devices, shards(): lax.all_to_all(spectrum, 'rows', split_axis=2, concat_axis=1, tiled=True)  90.7 us
    add x31, other arithmetic, combine(): first_records[3] * former + second_records[3] * latest  43 us
    add x31, other arithmetic, combine(): first_records[4] * former + second_records[4] * latest  38.9 us
    slice x5, local copies, waits for them, and re-layouts, combined_all(): tail = jax.tree.map(lambda part: part[1:], pieces)  37 us
  transfers between devices with their start and end apart: 10, of which 8 were waited for; matrix products, arithmetic and copies ran while one was open for 6% of the time, Pallas kernels for 0%

commit v1 on v0

v1 whole, which is shorter than its diff:
```python
import math

import jax
import jax.numpy as jnp
from jax import lax
from jax.experimental import pallas as pl
from jax.experimental.pallas import tpu as pltpu
from jax.sharding import PartitionSpec as P

NX = 4096
Y_WIN = 256
DEPTHS = 2048
MAXWIDTH = 3
TURN = NX * NX
HALF = 256
BLOCKS = 8
F32 = jnp.float32
BF16 = jnp.bfloat16
VMEM_LIMIT = 60 * 1024 * 1024


def cos_sin(turns):
    quarter = (turns + (1 << 21)) >> 22
    rest = turns - (quarter << 22)
    x = rest.astype(F32) * (2.0 * math.pi / TURN)
    x2 = x * x
    s = x * (1.0 + x2 * (-1.0 / 6 + x2 * (1.0 / 120 + x2 * (-1.0 / 5040 + x2 * (1.0 / 362880)))))
    c = 1.0 + x2 * (-0.5 + x2 * (1.0 / 24 + x2 * (-1.0 / 720 + x2 * (1.0 / 40320 - x2 * (1.0 / 3628800)))))
    odd = (quarter & 1) == 1
    cos_v = jnp.where(odd, s, c)
    sin_v = jnp.where(odd, c, s)
    cos_v = jnp.where(((quarter + 1) & 2) == 2, -cos_v, cos_v)
    sin_v = jnp.where((quarter & 2) == 2, -sin_v, sin_v)
    return cos_v, sin_v


def chirp_turns(z, s):
    square = s * s
    return (z * (square & (NX - 1)) + NX * ((z * (square >> 12)) & (NX - 1))) & (TURN - 1)


def pieces(value):
    high = value.astype(BF16)
    rest = value - high.astype(F32)
    mid = rest.astype(BF16)
    low = (rest - mid.astype(F32)).astype(BF16)
    return high, mid, low


def dot(a, b):
    return jnp.dot(a, b, preferred_element_type=F32)


def six(left, right):
    return (
        (dot(left[0], right[2]) + dot(left[2], right[0]) + dot(left[1], right[1]))
        + (dot(left[0], right[1]) + dot(left[1], right[0]))
        + dot(left[0], right[0])
    )


def pick_kernel(place_ref, spec_ref, out_ref):
    row_place = place_ref[1]
    q = lax.broadcasted_iota(jnp.int32, (128, 128), 0)
    lane = lax.broadcasted_iota(jnp.int32, (128, 128), 1)
    sort = (lane == (q >> 3) + 16 * (q & 7)).astype(F32).astype(BF16)
    i = lax.broadcasted_iota(jnp.int32, (HALF, HALF), 0)
    l = lax.broadcasted_iota(jnp.int32, (HALF, HALF), 1)
    source = jnp.where(row_place < BLOCKS, l, (HALF - l) & (HALF - 1))
    turn = (i == source).astype(F32).astype(BF16)
    both = []
    for c in range(2):
        picked = lax.dot_general(
            sort, spec_ref[c], (((1,), (1,)), ((), ())), preferred_element_type=F32
        )
        both.append(dot(picked.astype(BF16), turn).reshape(16, 8, HALF))
    out_ref[...] = jnp.concatenate(both, axis=1).astype(BF16)


def table_kernel(tab_ref, row_ref, twist_ref, base_c, base_s):
    b = pl.program_id(0)
    l = lax.broadcasted_iota(jnp.int32, (HALF, HALF), 0)
    y = lax.broadcasted_iota(jnp.int32, (HALF, HALF), 1)

    @pl.when(b == 0)
    def _():
        c, s = cos_sin((l * y & (NX - 1)) << 12)
        base_c[...] = c
        base_s[...] = s
        c, s = cos_sin((l * y & 255) << 16)
        for n, part in enumerate(pieces(c)):
            row_ref[0, n] = part
        for n, part in enumerate(pieces(s)):
            row_ref[1, n] = part
        r = lax.broadcasted_iota(jnp.int32, (16, HALF), 0)
        x = lax.broadcasted_iota(jnp.int32, (16, HALF), 1)
        c, s = cos_sin((r * x & (NX - 1)) << 12)
        twist_ref[0] = c * (1.0 / NX)
        twist_ref[1] = s * (1.0 / NX)

    lane = lax.broadcasted_iota(jnp.int32, (8, HALF), 1)
    c16, s16 = cos_sin((b * lane & 15) << 20)
    c16, s16 = c16[0:1], s16[0:1]
    cosine = base_c[...] * c16 - base_s[...] * s16
    sine = base_s[...] * c16 + base_c[...] * s16
    nyquist = (1 - 2 * (y & 1)).astype(F32)
    sine = jnp.where((l == 0) & (b == 0), nyquist, sine)
    for n, part in enumerate(pieces(cosine)):
        tab_ref[0, 0, n] = part
    for n, part in enumerate(pieces(sine)):
        tab_ref[0, 1, n] = part


def column_kernel(spec_ref, z_ref, tab_ref, out_ref, acc):
    b = pl.program_id(0)
    lane = lax.broadcasted_iota(jnp.int32, (32, HALF), 1)
    special = (lane == 0) & (b == 0)
    z = jnp.concatenate([z_ref[:, 0, :], z_ref[:, 0, :]], axis=1)
    s = jnp.where(special, NX // 2, b * HALF + lane)
    c_o, s_o = cos_sin(chirp_turns(z, s))
    s_o = -s_o
    c_e = jnp.where(special, 1.0, c_o)
    s_e = jnp.where(special, 0.0, s_o)

    lane16 = lax.broadcasted_iota(jnp.int32, (16, HALF), 1)
    plus = spec_ref[b].astype(F32)
    last = spec_ref[15 - b].astype(F32)
    first = spec_ref[jnp.where(b == 0, 8, 16 - b)].astype(F32)
    minus = jnp.where(lane16 == 0, first, last)
    corner = (lane16 == 0) & (b == 0)
    even = jnp.where(corner, plus, plus + minus)
    odd = plus - minus
    o_re = jnp.where(corner[:8], minus[:8], -odd[8:])
    o_im = jnp.where(corner[:8], minus[8:], odd[:8])
    e_re, e_im = even[:8], even[8:]

    def turned(re, im, c, s):
        c, s = c[:, None, :], s[:, None, :]
        t_re = (re[None] * c - im[None] * s).reshape(HALF, HALF)
        t_im = (re[None] * s + im[None] * c).reshape(HALF, HALF)
        return t_re, t_im

    parts = []
    for t, (re, im, c, s) in enumerate(((e_re, e_im, c_e, s_e), (o_re, o_im, c_o, s_o))):
        for half, value in enumerate(turned(re, im, c, s)):
            parts.append((half, six(pieces(value), [tab_ref[0, t, n] for n in range(3)])))
    for half in range(2):
        total = parts[half][1] + parts[half + 2][1]

        @pl.when(b == 0)
        def _():
            acc[half] = total

        @pl.when(b > 0)
        def _():
            acc[half] = acc[half] + total

    @pl.when(b == BLOCKS - 1)
    def _():
        for half in range(2):
            out_ref[:, half] = acc[half].reshape(32, 8, HALF)


def band_kernel(place_ref, in_ref, out_ref, re_s, im_s):
    row_place, z = place_ref[0], place_ref[1]
    v = row_place + 16 * lax.broadcasted_iota(jnp.int32, (8, HALF), 1)
    signed = jnp.where(v < NX // 2, v, v - NX)
    c, s = cos_sin(chirp_turns(z, signed))
    c, s = c[0:1], -s[0:1]
    re = in_ref[:, 0].reshape(HALF, HALF).T
    im = in_ref[:, 1].reshape(HALF, HALF).T
    re_s[...] = re * c - im * s
    im_s[...] = re * s + im * c
    zero = jnp.zeros((1, HALF), F32)
    for r in range(16):
        out_ref[r, 0:16] = re_s[16 * r : 16 * r + 16]
        out_ref[r, 16:32] = im_s[16 * r : 16 * r + 16]
        out_ref[r, 32:40] = jnp.zeros((8, HALF), F32)
        out_ref[r, 32:33] = re_s[16 * r - 1 : 16 * r] if r > 0 else zero
        out_ref[r, 33:34] = re_s[16 * r + 16 : 16 * r + 17] if r < 15 else zero
        out_ref[r, 36:37] = im_s[16 * r - 1 : 16 * r] if r > 0 else zero
        out_ref[r, 37:38] = im_s[16 * r + 16 : 16 * r + 17] if r < 15 else zero


def times_i(v):
    return -v[1], v[0]


def add(a, b):
    return a[0] + b[0], a[1] + b[1]


def sub(a, b):
    return a[0] - b[0], a[1] - b[1]


def times(a, c, s):
    return a[0] * c - a[1] * s, a[0] * s + a[1] * c


def four(a0, a1, a2, a3):
    p, q, m, n = add(a0, a2), add(a1, a3), sub(a0, a2), times_i(sub(a1, a3))
    return add(p, q), add(m, n), sub(p, q), sub(m, n)


def sixteen(a):
    inner = [four(a[r], a[r + 4], a[r + 8], a[r + 12]) for r in range(4)]
    out = [None] * 16
    for k in range(4):
        row = []
        for r in range(4):
            t = r * k
            v = inner[r][k]
            row.append(v if t == 0 else times(v, math.cos(math.pi * t / 8), math.sin(math.pi * t / 8)))
        for m, v in enumerate(four(*row)):
            out[k + 4 * m] = v
    return out


def row_kernel(width_ref, gain_ref, in_ref, row_ref, twist_ref, out_ref, a_s, b_s, power):
    left = pieces(in_ref[...].reshape(640, HALF))
    a_s[...] = six(left, [row_ref[0, n] for n in range(3)]).reshape(16, 40, HALF)
    b_s[...] = six(left, [row_ref[1, n] for n in range(3)]).reshape(16, 40, HALF)
    for half in range(2):
        lanes = slice(128 * half, 128 * half + 128)
        for band in range(3):
            values = []
            for r in range(16):
                if band < 2:
                    top, low = slice(8 * band, 8 * band + 8), slice(16 + 8 * band, 24 + 8 * band)
                    re = a_s[r, top, lanes] - b_s[r, low, lanes]
                    im = b_s[r, top, lanes] + a_s[r, low, lanes]
                else:
                    a, b = a_s[r, 32:40, lanes], b_s[r, 32:40, lanes]
                    re = a - pltpu.roll(b, 4, 0)
                    im = b + pltpu.roll(a, 4, 0)
                values.append(times((re, im), twist_ref[0, r : r + 1, lanes], twist_ref[1, r : r + 1, lanes]))
            for k, (re, im) in enumerate(sixteen(values)):
                target = 2 * k + half
                if band < 2:
                    out_ref[target, 1, 8 * band : 8 * band + 8] = re
                    out_ref[target, 2, 8 * band : 8 * band + 8] = im
                power[8 * band : 8 * band + 8, 128 * target : 128 * target + 128] = re * re + im * im
    here = power[0:16]
    row = lax.broadcasted_iota(jnp.int32, (16, NX), 0)
    lane = lax.broadcasted_iota(jnp.int32, (16, NX), 1)
    up = jnp.where(row == 0, power[16:17], pltpu.roll(here, 1, 0))
    down = jnp.where(row == 15, power[17:18], pltpu.roll(here, 15, 0))

    def moved(v, offset):
        if offset > 0:
            return jnp.where(lane < NX - offset, pltpu.roll(v, NX - offset, 1), 0.0)
        return jnp.where(lane >= -offset, pltpu.roll(v, -offset, 1), 0.0)

    vertical = up + 2.0 * here + down
    step = down - up
    across = moved(vertical, 1) - moved(vertical, -1)
    downward = moved(step, -1) + 2.0 * step + moved(step, 1)
    energy = across * across + downward * downward
    radius = width_ref[0]
    total = energy
    for offset in range(1, MAXWIDTH + 1):
        inside = (offset <= radius).astype(F32)
        total = total + inside * (moved(energy, -offset) + moved(energy, offset))
    smoothed = total / (2 * radius + 1).astype(F32)
    scores = gain_ref[0] * jnp.log(1.0 + smoothed)
    for target in range(32):
        out_ref[target, 0] = scores[:, 128 * target : 128 * target + 128]


def merge_kernel(in_ref, z_ref, depth_ref, focus_ref):
    peak = jnp.max(in_ref[:, 0], axis=0)
    weights = [jnp.exp(in_ref[p, 0] - peak) for p in range(32)]
    total = sum(weights[1:], weights[0])
    depth = sum(w * (z_ref[p].astype(F32) * (1.0 / DEPTHS)) for p, w in enumerate(weights))
    depth_ref[...] = depth / total
    focus_ref[0] = sum(w * in_ref[p, 1] for p, w in enumerate(weights)) / total
    focus_ref[1] = sum(w * in_ref[p, 2] for p, w in enumerate(weights)) / total


def params():
    return pltpu.CompilerParams(vmem_limit_bytes=VMEM_LIMIT)


def whole(shape):
    return pl.BlockSpec(shape, lambda *_: (0,) * len(shape))


def cost(flops, size):
    return pl.CostEstimate(flops=flops, bytes_accessed=size, transcendentals=0)


def shards(spectrum, plane_index, kernel_width, focus_gain):
    depth_place = lax.axis_index("depth")
    row_place = lax.axis_index("rows")
    z_mine = jnp.broadcast_to(plane_index[:, None, None], (32, 1, 128))
    z_all = lax.all_to_all(z_mine, "depth", split_axis=0, concat_axis=0, tiled=True)

    picked = pl.pallas_call(
        pick_kernel,
        grid_spec=pltpu.PrefetchScalarGridSpec(
            num_scalar_prefetch=1,
            grid=(1,),
            in_specs=[pl.BlockSpec((2, HALF, 128), lambda i, place: (0, 0, place[0]))],
            out_specs=whole((16, 16, HALF)),
        ),
        out_shape=jax.ShapeDtypeStruct((16, 16, HALF), BF16),
        compiler_params=params(),
        cost_estimate=cost(50_000_000, 300_000),
        name="pick",
    )(jnp.stack([depth_place, row_place]).astype(jnp.int32), spectrum)
    columns = lax.all_to_all(picked, "rows", split_axis=0, concat_axis=0, tiled=True)

    tables, row_table, twist = pl.pallas_call(
        table_kernel,
        grid=(BLOCKS,),
        in_specs=[],
        out_specs=[
            pl.BlockSpec((1, 2, 3, HALF, HALF), lambda b: (b, 0, 0, 0, 0)),
            whole((2, 3, HALF, HALF)),
            whole((2, 16, HALF)),
        ],
        out_shape=[
            jax.ShapeDtypeStruct((BLOCKS, 2, 3, HALF, HALF), BF16),
            jax.ShapeDtypeStruct((2, 3, HALF, HALF), BF16),
            jax.ShapeDtypeStruct((2, 16, HALF), F32),
        ],
        scratch_shapes=[pltpu.VMEM((HALF, HALF), F32), pltpu.VMEM((HALF, HALF), F32)],
        compiler_params=params(),
        cost_estimate=cost(30_000_000, 7_000_000),
        name="tables",
    )()

    strips = pl.pallas_call(
        column_kernel,
        grid=(BLOCKS,),
        in_specs=[
            whole((16, 16, HALF)),
            whole((32, 1, 128)),
            pl.BlockSpec((1, 2, 3, HALF, HALF), lambda b: (b, 0, 0, 0, 0)),
        ],
        out_specs=whole((32, 2, 8, HALF)),
        out_shape=jax.ShapeDtypeStruct((32, 2, 8, HALF), F32),
        scratch_shapes=[pltpu.VMEM((2, HALF, HALF), F32)],
        compiler_params=params(),
        cost_estimate=cost(6_500_000_000, 8_000_000),
        name="columns",
    )(columns, z_all, tables)
    by_plane = lax.all_to_all(strips, "depth", split_axis=0, concat_axis=0, tiled=True)

    bands = pl.pallas_call(
        band_kernel,
        grid_spec=pltpu.PrefetchScalarGridSpec(
            num_scalar_prefetch=1,
            grid=(1,),
            in_specs=[whole((32, 2, 8, HALF))],
            out_specs=whole((16, 40, HALF)),
            scratch_shapes=[pltpu.VMEM((HALF, HALF), F32), pltpu.VMEM((HALF, HALF), F32)],
        ),
        out_shape=jax.ShapeDtypeStruct((16, 40, HALF), F32),
        compiler_params=params(),
        cost_estimate=cost(1_000_000, 1_200_000),
        name="bands",
    )(jnp.stack([row_place.astype(jnp.int32), plane_index[0]]), by_plane)
    rows_in = lax.all_to_all(bands, "rows", split_axis=0, concat_axis=0, tiled=True)

    smem = pl.BlockSpec(memory_space=pltpu.SMEM)
    records = pl.pallas_call(
        row_kernel,
        in_specs=[
            smem,
            smem,
            whole((16, 40, HALF)),
            whole((2, 3, HALF, HALF)),
            whole((2, 16, HALF)),
        ],
        out_specs=whole((32, 3, 16, 128)),
        out_shape=jax.ShapeDtypeStruct((32, 3, 16, 128), F32),
        scratch_shapes=[
            pltpu.VMEM((16, 40, HALF), F32),
            pltpu.VMEM((16, 40, HALF), F32),
            pltpu.VMEM((24, NX), F32),
        ],
        compiler_params=params(),
        cost_estimate=cost(1_000_000_000, 2_200_000),
        name="rows",
    )(kernel_width, focus_gain, rows_in, row_table, twist)
    merged = lax.all_to_all(records, "depth", split_axis=0, concat_axis=0, tiled=True)

    depth_map, focused = pl.pallas_call(
        merge_kernel,
        in_specs=[whole((32, 3, 16, 128)), whole((32, 1, 128))],
        out_specs=[whole((16, 128)), whole((2, 16, 128))],
        out_shape=[
            jax.ShapeDtypeStruct((16, 128), F32),
            jax.ShapeDtypeStruct((2, 16, 128), F32),
        ],
        compiler_params=params(),
        cost_estimate=cost(1_000_000, 900_000),
        name="merge",
    )(merged, z_all)
    return depth_map, focused


def solution(mesh):
    return jax.shard_map(
        shards,
        mesh=mesh,
        in_specs=(P(None, "rows", None), P("depth"), P("depth"), P("depth")),
        out_specs=(P("rows", "depth"), P(None, "rows", "depth")),
        check_vma=False,
    )
```

time: 857 us -> 139 us (0.16)
  waiting for transfers between devices: 584 us -> 43.8 us
  other arithmetic: 97.1 us -> 1.2 us
  local copies, waits for them, and re-layouts: 70.1 us -> 2.92 us
  matrix products: 54.1 us -> 0 us
  Pallas kernels: 0 us -> 29.6 us
  blocking collectives: 0 us -> 26.7 us
  between operations: 16.6 us -> 2.61 us
    all_gather x5 -> x0, waiting for transfers between devices: 480 us -> none  [combined_all(): pieces = jax.tree.map(lambda part: lax.all_gather(part, axis), value)]
    add x67 -> x0, other arithmetic: 82.6 us -> none  [the longest x31 43 us: combine(): first_records[3] * former + second_records[3] * latest]
    all_to_all x3 -> x4, waiting for transfers between devices: 99.7 us -> 43.8 us  [the longest x1 18.6 us: shards(): lax.all_to_all(bands, 'rows', split_axis=0, concat_axis=0, tiled=True)]
    dot_general x16 -> x0, matrix products: 54.1 us -> none  [the longest x4 14.6 us: complex_einsum(): product(imag_part, table_real)]
    slice x6 -> x0, local copies, waits for them, and re-layouts: 37.1 us -> none  [the longest x5 37 us: combined_all(): tail = jax.tree.map(lambda part: part[1:], pieces)]
    pallas_call x0 -> x6, Pallas kernels: none -> 29.6 us  [the longest x1 12.2 us: shards(): pl.pallas_call(column_kernel, grid=(BLOCKS,), in_specs=[whole((16, 16, HA...]
    all_to_all x0 -> x1, blocking collectives: none -> 26.7 us  [shards(): lax.all_to_all(records, 'depth', split_axis=0, concat_axis=0, tiled=True)]
    convert_element_type x2 -> x0, local copies, waits for them, and re-layouts: 10.8 us -> none  [the longest x1 5.45 us: rotate(): real_in = spectra[0].astype(jnp.float32)]
  transfers between devices with their start and end apart: 10 -> 4, of which waited for: 8 -> 4; matrix products, arithmetic and copies ran while one was open for 6% -> 1% of each run, Pallas kernels for 0% -> 6%
where the time goes in v1:
time: 139 us
  waiting for transfers between devices  43.8 us (32%)
  starting transfers between devices  31.9 us (23%)
  Pallas kernels  29.6 us (21%)
  blocking collectives  26.7 us (19%)
  local copies, waits for them, and re-layouts  2.92 us (2%)
  between operations  2.61 us (2%)
    all_to_all x1, blocking collectives, shards(): lax.all_to_all(records, 'depth', split_axis=0, concat_axis=0, tiled=True)  26.7 us
    all_to_all x1, waiting for transfers between devices, shards(): lax.all_to_all(bands, 'rows', split_axis=0, concat_axis=0, tiled=True)  18.6 us
    all_to_all x1, waiting for transfers between devices, shards(): lax.all_to_all(strips, 'depth', split_axis=0, concat_axis=0, tiled=True)  16.7 us
    all_to_all x1, starting transfers between devices, shards(): lax.all_to_all(z_mine, 'depth', split_axis=0, concat_axis=0, tiled=True)  13.7 us
    pallas_call x1, Pallas kernels, shards(): pl.pallas_call(column_kernel, grid=(BLOCKS,), in_specs=[whole((16, 16, HA...  12.2 us
    all_to_all x1, starting transfers between devices, shards(): lax.all_to_all(picked, 'rows', split_axis=0, concat_axis=0, tiled=True)  9.22 us
    pallas_call x1, Pallas kernels, shards(): pl.pallas_call(table_kernel, grid=(BLOCKS,), in_specs=[], out_specs=[pl.B...  5.8 us
    all_to_all x1, waiting for transfers between devices, shards(): lax.all_to_all(z_mine, 'depth', split_axis=0, concat_axis=0, tiled=True)  5.36 us
  transfers between devices with their start and end apart: 4, of which 4 were waited for; matrix products, arithmetic and copies ran while one was open for 1% of the time, Pallas kernels for 6%

profile of v1, /device:TPU:1, one launch (start us, length us, event | category | flops | bytes accessed | tf_op | source)
XLA Modules:
  0.0 138.7 jit_solution(2123364466415324116)
XLA Ops:
  1.3 0.6 broadcast_in_dim.9
  1.9 13.7 %all-to-all-start.1 = ((s32[32,1,128]{2,1,0:T(1,128)}), s32[32,1,128]{2,1,0:T(1,128)S(1)}, u32[]{:S(2)}, u32[]{:S(2)}) async-start(s32[32,1,128]{2,1,0:T(1,128)} %broadcast_in_dim.9), calls=%async_computation.1 | async-start | bytes 32768 | tf_op jit(solution)/shard_map/all_to_all | solution.py:297
  15.6 0.6 pad_add_fusion.1.place_ref
  16.2 2.6 %pick.1 = bf16[16,16,256]{2,1,0:T(8,128)(2,1)} custom-call(s32[2]{0:T(128)} %pad_add_fusion.1.place_ref, bf16[2,256,4096]{2,1,0:T(8,128)(2,1)} %spec_ref.1), custom_call_target="tpu_custom_call" | custom-call | flops 50000000 | bytes 300000 | tf_op jit(solution)/shard_map/pick/pallas_call | solution.py:299
  18.8 5.4 %all-to-all-done.1.z_ref = s32[32,1,128]{2,1,0:T(1,128)S(1)} async-done(((s32[32,1,128]{2,1,0:T(1,128)}), s32[32,1,128]{2,1,0:T(1,128)S(1)}, u32[]{:S(2)}, u32[]{:S(2)}) %all-to-all-start.1) | async-done | bytes 16416 | tf_op jit(solution)/shard_map/all_to_all | solution.py:297
  24.1 0.0 copy-start.3
  24.1 9.2 %all-to-all-start = ((bf16[16,16,256]{2,1,0:T(8,128)(2,1)}), bf16[16,16,256]{2,1,0:T(8,128)(2,1)S(1)}, u32[]{:S(2)}, u32[]{:S(2)}) async-start(bf16[16,16,256]{2,1,0:T(8,128)(2,1)} %pick.1), calls=%async_computation | async-start | bytes 262144 | tf_op jit(solution)/shard_map/all_to_all | solution.py:312
  33.4 5.8 %tables.1 = (bf16[8,2,3,256,256]{4,3,2,1,0:T(8,128)(2,1)}, bf16[2,3,256,256]{3,2,1,0:T(8,128)(2,1)}, f32[2,16,256]{2,1,0:T(8,128)}) custom-call(), custom_call_target="tpu_custom_call" | custom-call | flops 30000000 | bytes 7000000 | tf_op jit(solution)/shard_map/tables/pallas_call | solution.py:314
  39.2 3.1 %all-to-all-done.spec_ref = bf16[16,16,256]{2,1,0:T(8,128)(2,1)S(1)} async-done(((bf16[16,16,256]{2,1,0:T(8,128)(2,1)}), bf16[16,16,256]{2,1,0:T(8,128)(2,1)S(1)}, u32[]{:S(2)}, u32[]{:S(2)}) %all-to-all-start) | async-done | bytes 131104 | tf_op jit(solution)/shard_map/all_to_all | solution.py:312
  42.2 0.0 copy-start.2
  42.2 0.0 copy-done.3
  42.2 0.6 copy-done.2
  42.9 12.2 %columns.1 = f32[32,2,8,256]{3,2,1,0:T(8,128)} custom-call(bf16[16,16,256]{2,1,0:T(8,128)(2,1)} %copy-done.2, s32[32,1,128]{2,1,0:T(1,128)} %copy-done.3, bf16[8,2,3,256,256]{4,3,2,1,0:T(8,128)(2,1)} %get-tuple-element.5.tab_ref), custom_call_target="tpu_custom_call" | custom-call | flops 6499999744 | bytes 8000000 | tf_op jit(solution)/shard_map/columns/pallas_call | solution.py:334
  55.1 3.9 %all-to-all-start.2 = ((f32[32,2,8,256]{3,2,1,0:T(8,128)}), f32[32,2,8,256]{3,2,1,0:T(8,128)S(1)}, u32[]{:S(2)}, u32[]{:S(2)}) async-start(f32[32,2,8,256]{3,2,1,0:T(8,128)} %columns.1), calls=%async_computation.2 | async-start | bytes 1048576 | tf_op jit(solution)/shard_map/all_to_all | solution.py:349
  59.0 0.6 pad_add_fusion.place_ref
  59.6 16.7 %all-to-all-done.2.in_ref = f32[32,2,8,256]{3,2,1,0:T(8,128)S(1)} async-done(((f32[32,2,8,256]{3,2,1,0:T(8,128)}), f32[32,2,8,256]{3,2,1,0:T(8,128)S(1)}, u32[]{:S(2)}, u32[]{:S(2)}) %all-to-all-start.2) | async-done | bytes 524320 | tf_op jit(solution)/shard_map/all_to_all | solution.py:349
  76.3 0.0 copy-start
  76.3 0.8 copy-done
  77.1 2.8 %bands.1 = f32[16,40,256]{2,1,0:T(8,128)} custom-call(s32[2]{0:T(128)} %pad_add_fusion.place_ref, f32[32,2,8,256]{3,2,1,0:T(8,128)} %copy-done), custom_call_target="tpu_custom_call" | custom-call | flops 1000000 | bytes 1200000 | tf_op jit(solution)/shard_map/bands/pallas_call | solution.py:351
  79.9 5.1 %all-to-all-start.3 = ((f32[16,40,256]{2,1,0:T(8,128)}), f32[16,40,256]{2,1,0:T(8,128)S(1)}, u32[]{:S(2)}, u32[]{:S(2)}) async-start(f32[16,40,256]{2,1,0:T(8,128)} %bands.1), calls=%async_computation.3 | async-start | bytes 1310720 | tf_op jit(solution)/shard_map/all_to_all | solution.py:365
  86.3 18.6 %all-to-all-done.3.in_ref = f32[16,40,256]{2,1,0:T(8,128)S(1)} async-done(((f32[16,40,256]{2,1,0:T(8,128)}), f32[16,40,256]{2,1,0:T(8,128)S(1)}, u32[]{:S(2)}, u32[]{:S(2)}) %all-to-all-start.3) | async-done | bytes 655392 | tf_op jit(solution)/shard_map/all_to_all | solution.py:365
  105.0 0.0 copy-start.1
  105.0 0.9 copy-done.1
  105.8 4.4 %rows.1 = f32[32,3,16,128]{3,2,1,0:T(8,128)} custom-call(s32[1]{0:T(128)S(6)} %copy.7.width_ref, f32[1]{0:T(128)S(6)} %copy.8.gain_ref, f32[16,40,256]{2,1,0:T(8,128)} %copy-done.1, bf16[2,3,256,256]{3,2,1,0:T(8,128)(2,1)} %get-tuple-element.6.row_ref, f32[2,16,256]{2,1,0:T(8,128)} %get-tuple-element.7.twist_ref), custom_call_target="tpu_custom_call" | custom-call | flops 1000000000 | bytes 2200000 | tf_op jit(solution)/shard_map/rows/pallas_call | solution.py:368
  110.2 26.7 %all_to_all.25.in_ref = f32[32,3,16,128]{3,2,1,0:T(8,128)} all-to-all(f32[32,3,16,128]{3,2,1,0:T(8,128)} %rows.1), channel_id=1, replica_groups=mesh['depth'=32,'rows'=16] {'depth'}, dimensions={0} | all-to-all | bytes 1572864 | tf_op jit(solution)/shard_map/all_to_all | solution.py:388
  136.8 1.9 %merge.1 = (f32[16,128]{1,0:T(8,128)}, f32[2,16,128]{2,1,0:T(8,128)}) custom-call(f32[32,3,16,128]{3,2,1,0:T(8,128)} %all_to_all.25.in_ref, s32[32,1,128]{2,1,0:T(1,128)} %copy-done.3), custom_call_target="tpu_custom_call" | custom-call | flops 1000000 | bytes 900000 | tf_op jit(solution)/shard_map/merge/pallas_call | solution.py:390
Async XLA Ops:
  1.9 22.2 %all-to-all-start.1 = ((s32[32,1,128]{2,1,0:T(1,128)}), s32[32,1,128]{2,1,0:T(1,128)S(1)}, u32[]{:S(2)}, u32[]{:S(2)}) async-start(s32[32,1,128]{2,1,0:T(1,128)} %broadcast_in_dim.9), calls=%async_computation.1 | async-start | bytes 32768 | tf_op jit(solution)/shard_map/all_to_all | solution.py:297
  24.1 18.1 %copy-start.3 = (s32[32,1,128]{2,1,0:T(1,128)}, s32[32,1,128]{2,1,0:T(1,128)S(1)}, u32[]{:S(2)}) copy-start(s32[32,1,128]{2,1,0:T(1,128)S(1)} %all-to-all-done.1.z_ref) | copy-start | bytes 49156
  24.1 18.1 %all-to-all-start = ((bf16[16,16,256]{2,1,0:T(8,128)(2,1)}), bf16[16,16,256]{2,1,0:T(8,128)(2,1)S(1)}, u32[]{:S(2)}, u32[]{:S(2)}) async-start(bf16[16,16,256]{2,1,0:T(8,128)(2,1)} %pick.1), calls=%async_computation | async-start | bytes 262144 | tf_op jit(solution)/shard_map/all_to_all | solution.py:312
  42.2 0.7 copy-start.2
  55.1 21.2 %all-to-all-start.2 = ((f32[32,2,8,256]{3,2,1,0:T(8,128)}), f32[32,2,8,256]{3,2,1,0:T(8,128)S(1)}, u32[]{:S(2)}, u32[]{:S(2)}) async-start(f32[32,2,8,256]{3,2,1,0:T(8,128)} %columns.1), calls=%async_computation.2 | async-start | bytes 1048576 | tf_op jit(solution)/shard_map/all_to_all | solution.py:349
  76.3 0.8 copy-start
  79.9 25.0 %all-to-all-start.3 = ((f32[16,40,256]{2,1,0:T(8,128)}), f32[16,40,256]{2,1,0:T(8,128)S(1)}, u32[]{:S(2)}, u32[]{:S(2)}) async-start(f32[16,40,256]{2,1,0:T(8,128)} %bands.1), calls=%async_computation.3 | async-start | bytes 1310720 | tf_op jit(solution)/shard_map/all_to_all | solution.py:365
  105.0 0.9 copy-start.1

commit v2 on v1

v2 whole, which is shorter than its diff:
```python
import math

import jax
import jax.numpy as jnp
from jax import lax
from jax.experimental import pallas as pl
from jax.experimental.pallas import tpu as pltpu
from jax.sharding import PartitionSpec as P

NX = 4096
Y_WIN = 256
DEPTHS = 2048
MAXWIDTH = 3
TURN = NX * NX
HALF = 256
BLOCKS = 8
F32 = jnp.float32
BF16 = jnp.bfloat16
PIECES = 2
ALL = ("depth", "rows")


def cos_sin(turns):
    quarter = (turns + (1 << 21)) >> 22
    rest = turns - (quarter << 22)
    x = rest.astype(F32) * (2.0 * math.pi / TURN)
    x2 = x * x
    s = x * (1.0 + x2 * (-1.0 / 6 + x2 * (1.0 / 120 + x2 * (-1.0 / 5040 + x2 * (1.0 / 362880)))))
    c = 1.0 + x2 * (-0.5 + x2 * (1.0 / 24 + x2 * (-1.0 / 720 + x2 * (1.0 / 40320 - x2 * (1.0 / 3628800)))))
    odd = (quarter & 1) == 1
    cos_v = jnp.where(odd, s, c)
    sin_v = jnp.where(odd, c, s)
    cos_v = jnp.where(((quarter + 1) & 2) == 2, -cos_v, cos_v)
    sin_v = jnp.where((quarter & 2) == 2, -sin_v, sin_v)
    return cos_v, sin_v


def chirp_turns(z, s):
    square = s * s
    return (z * (square & (NX - 1)) + NX * ((z * (square >> 12)) & (NX - 1))) & (TURN - 1)


def pieces(value):
    out = []
    for n in range(PIECES):
        out.append(value.astype(BF16))
        if n < PIECES - 1:
            value = value - out[-1].astype(F32)
    return out


def dot(a, b):
    return jnp.dot(a, b, preferred_element_type=F32)


def product(left, right):
    if PIECES == 2:
        return (dot(left[0], right[1]) + dot(left[1], right[0])) + dot(left[0], right[0])
    return (
        (dot(left[0], right[2]) + dot(left[2], right[0]) + dot(left[1], right[1]))
        + (dot(left[0], right[1]) + dot(left[1], right[0]))
        + dot(left[0], right[0])
    )


def places():
    d, r = lax.axis_index("depth"), lax.axis_index("rows")
    return d, r, (r - d) & 15


def swapped(parts, group):
    count = len(parts)
    lane = lax.broadcasted_iota(jnp.int32, parts[0].shape, 1)
    parts = list(parts)
    step = 1
    while step < count:
        low = ((lane // group) & step) == 0
        for i in range(count):
            if i & step == 0:
                x, y = parts[i], parts[i + step]
                parts[i] = jnp.where(low, x, pltpu.roll(y, group * step, 1))
                parts[i + step] = jnp.where(low, pltpu.roll(x, 128 - group * step, 1), y)
        step *= 2
    return parts


def pick_kernel(z_ref, width_ref, gain_ref, spec_ref, out_ref, buf, sem):
    d, r, j = places()
    copy = pltpu.make_async_copy(
        spec_ref.at[:, pl.ds(pl.multiple_of(128 * (d >> 4), 128), 128), pl.ds(pl.multiple_of(256 * j, 256), 256)],
        buf,
        sem,
    )
    copy.start()
    q = lax.broadcasted_iota(jnp.int32, (256, 256), 0)
    lane = lax.broadcasted_iota(jnp.int32, (256, 256), 1)
    target = q >> 3
    sort = (lane == (target & 15) + 128 * (target >> 4) + 16 * (q & 7)).astype(F32).astype(BF16)
    i = lax.broadcasted_iota(jnp.int32, (128, 128), 0)
    l = lax.broadcasted_iota(jnp.int32, (128, 128), 1)
    source = jnp.where(r < BLOCKS, l, (128 - l) & 127)
    turn = (i == source).astype(F32).astype(BF16)
    row = lax.broadcasted_iota(jnp.int32, (8, 128), 0)
    gain = jnp.full((8, 128), gain_ref[0], F32)
    high = gain.astype(BF16).astype(F32)
    mid = (gain - high).astype(BF16).astype(F32)
    z = z_ref[0]
    extra = jnp.zeros((8, 128), F32)
    values = ((z & ~31).astype(F32), (z & 31).astype(F32), width_ref[0].astype(F32), high, mid, gain - high - mid)
    for n, value in enumerate(values):
        extra = jnp.where(row == n, value, extra)
    copy.wait()
    both = []
    for c in range(2):
        picked = lax.dot_general(sort, buf[c], (((1,), (1,)), ((), ())), preferred_element_type=F32)
        both.append(dot(picked.astype(BF16), turn).reshape(32, 8, 128))
    both.append(jnp.broadcast_to(extra[None], (32, 8, 128)))
    out_ref[...] = jnp.concatenate(both, axis=1).astype(BF16)


def table_kernel(tab_ref, row_ref, twist_ref, base_c, base_s):
    b = pl.program_id(0)
    l = lax.broadcasted_iota(jnp.int32, (HALF, HALF), 0)
    y = lax.broadcasted_iota(jnp.int32, (HALF, HALF), 1)

    @pl.when(b == 0)
    def _():
        c, s = cos_sin((l * y & (NX - 1)) << 12)
        base_c[...] = c
        base_s[...] = s
        number = 16 * (l & 15) + 8 * ((l >> 4) & 1) + 4 * (l >> 7) + ((l >> 5) & 3)
        c, s = cos_sin((number * y & 255) << 16)
        for n, part in enumerate(pieces(c)):
            row_ref[0, n] = part
        for n, part in enumerate(pieces(s)):
            row_ref[1, n] = part
        k = lax.broadcasted_iota(jnp.int32, (16, HALF), 0)
        x = lax.broadcasted_iota(jnp.int32, (16, HALF), 1)
        c, s = cos_sin(((k * x - 256 * k * x) & (NX - 1)) << 12)
        twist_ref[0] = c * (1.0 / NX)
        twist_ref[1] = s * (1.0 / NX)

    lane = lax.broadcasted_iota(jnp.int32, (8, HALF), 1)
    c16, s16 = cos_sin((b * lane & 15) << 20)
    c16, s16 = c16[0:1], s16[0:1]
    cosine = base_c[...] * c16 - base_s[...] * s16
    sine = base_s[...] * c16 + base_c[...] * s16
    nyquist = (1 - 2 * (y & 1)).astype(F32)
    sine = jnp.where((l == 0) & (b == 0), nyquist, sine)
    for n, part in enumerate(pieces(cosine)):
        tab_ref[0, 0, n] = part
    for n, part in enumerate(pieces(sine)):
        tab_ref[0, 1, n] = part


def column_kernel(spec_ref, tab_ref, out_ref, par_ref, acc, par_s, bands):
    b = pl.program_id(0)
    d, r, j = places()

    @pl.when(b == 0)
    def _():
        par_s[...] = spec_ref[:, 16:24].astype(F32).reshape(256, 128)
        rows = [par_s[pl.ds(n, 32, stride=8), :] for n in range(6)]
        par_ref[0] = rows[0] + rows[1]
        par_ref[1] = rows[2]
        par_ref[2] = rows[3] + rows[4] + rows[5]

    lane = lax.broadcasted_iota(jnp.int32, (32, HALF), 1)
    special = (lane == 0) & (b == 0)
    z = par_ref[0].astype(jnp.int32)
    z2 = jnp.concatenate([z, z], axis=1)
    s = jnp.where(special, NX // 2, b * HALF + lane)
    c_o, s_o = cos_sin(chirp_turns(z2, s))
    s_o = -s_o
    c_e = jnp.where(special, 1.0, c_o)
    s_e = jnp.where(special, 0.0, s_o)

    def block(n):
        return spec_ref[(((n >> 1) - j) & 15) + 16 * (n & 1), 0:16].astype(F32)

    lane16 = lax.broadcasted_iota(jnp.int32, (16, HALF), 1)
    plus = jnp.concatenate([block(2 * b), block(2 * b + 1)], axis=1)
    middle = block(31 - 2 * b)
    last = jnp.concatenate([middle, block(30 - 2 * b)], axis=1)
    first = jnp.concatenate([block(jnp.where(b == 0, 16, 32 - 2 * b)), middle], axis=1)
    minus = jnp.where((lane16 & 127) == 0, first, last)
    corner = (lane16 == 0) & (b == 0)
    even = jnp.where(corner, plus, plus + minus)
    odd = plus - minus
    o_re = jnp.where(corner[:8], minus[:8], -odd[8:])
    o_im = jnp.where(corner[:8], minus[8:], odd[:8])
    e_re, e_im = even[:8], even[8:]

    def turned(re, im, c, s):
        re, im = re[:, None, :], im[:, None, :]
        t_re = (re * c[None] - im * s[None]).reshape(HALF, HALF)
        t_im = (re * s[None] + im * c[None]).reshape(HALF, HALF)
        return t_re, t_im

    parts = []
    for t, (re, im, c, s) in enumerate(((e_re, e_im, c_e, s_e), (o_re, o_im, c_o, s_o))):
        for value in turned(re, im, c, s):
            parts.append(product(pieces(value), [tab_ref[0, t, n] for n in range(PIECES)]))
    for half in range(2):
        total = parts[half] + parts[half + 2]

        @pl.when(b == 0)
        def _():
            acc[half] = total

        @pl.when(b > 0)
        def _():
            acc[half] = acc[half] + total

    @pl.when(b == BLOCKS - 1)
    def _():
        lane = lax.broadcasted_iota(jnp.int32, (8, 128), 1)
        group = (lane >> 2) & 3
        plane = z[0:8]
        for n in range(1, 4):
            plane = jnp.where(group == n, z[8 * n : 8 * n + 8], plane)
        v = 256 * j + 128 * (d >> 4) + 16 * (lane >> 4) + (d & 15)
        c, s = cos_sin(chirp_turns(plane, jnp.where(v < NX // 2, v, v - NX)))
        s = -s
        for half in range(2):
            cols = slice(128 * half, 128 * half + 128)
            for part in range(2):
                for n, v in enumerate(swapped([acc[part, 8 * i : 8 * i + 8, cols] for i in range(32)], 4)):
                    bands[part, 32 * half + n] = v
        for n in range(64):
            re, im = bands[0, n], bands[1, n]
            bands[0, n] = re * c - im * s
            bands[1, n] = re * s + im * c
        slot = lane & 3
        for n in range(64):
            zero = jnp.zeros((8, 128), F32)
            above = [bands[part, n - 1] if n > 0 else zero for part in range(2)]
            below = [bands[part, n + 1] if n < 63 else zero for part in range(2)]
            rim = jnp.where(
                slot < 2,
                jnp.where(slot == 0, pltpu.roll(above[0], 125, 1), pltpu.roll(below[0], 1, 1)),
                jnp.where(slot == 2, pltpu.roll(above[1], 127, 1), pltpu.roll(below[1], 3, 1)),
            )
            item = 3 * ((n & 3) * 16 + (n >> 2))
            out_ref[pl.ds(item, 8, stride=192), :] = bands[0, n]
            out_ref[pl.ds(item + 1, 8, stride=192), :] = bands[1, n]
            out_ref[pl.ds(item + 2, 8, stride=192), :] = rim


def times_i(v):
    return -v[1], v[0]


def add(a, b):
    return a[0] + b[0], a[1] + b[1]


def sub(a, b):
    return a[0] - b[0], a[1] - b[1]


def times(a, c, s):
    return a[0] * c - a[1] * s, a[0] * s + a[1] * c


def four(a0, a1, a2, a3):
    p, q, m, n = add(a0, a2), add(a1, a3), sub(a0, a2), times_i(sub(a1, a3))
    return add(p, q), add(m, n), sub(p, q), sub(m, n)


def sixteen(a):
    inner = [four(a[r], a[r + 4], a[r + 8], a[r + 12]) for r in range(4)]
    out = [None] * 16
    for k in range(4):
        row = []
        for r in range(4):
            t = r * k
            v = inner[r][k]
            row.append(v if t == 0 else times(v, math.cos(math.pi * t / 8), math.sin(math.pi * t / 8)))
        for m, v in enumerate(four(*row)):
            out[k + 4 * m] = v
    return out


def row_kernel(in_ref, par_ref, row_ref, twist_ref, out_ref, x_s, a_s, b_s, power, re_s, im_s):
    d, _, _ = places()
    g = d >> 2
    for quad in range(4):
        for piece in range(3):
            rows = []
            for n in range(4):
                for half in range(2):
                    start = 48 * (4 * quad + n + 16 * half) + piece
                    rows.append(in_ref[pl.ds(start, 16, stride=3), :])
            turned = jnp.concatenate(rows, axis=0).T
            for a in range(2):
                parts = swapped([turned[64 * a + 16 * n : 64 * a + 16 * n + 16] for n in range(4)], 32)
                for n, part in enumerate(parts):
                    x_s[4 * quad + n, 16 * piece : 16 * piece + 16, 128 * a : 128 * a + 128] = part
    left = pieces(x_s[...].reshape(768, HALF))
    a_s[...] = product(left, [row_ref[0, n] for n in range(PIECES)]).reshape(16, 48, HALF)
    b_s[...] = product(left, [row_ref[1, n] for n in range(PIECES)]).reshape(16, 48, HALF)
    for half in range(2):
        lanes = slice(128 * half, 128 * half + 128)
        for band in range(4):
            here = slice(8 * band, 8 * band + 8)
            values = []
            for k in range(16):
                if band < 2:
                    low = slice(16 + 8 * band, 24 + 8 * band)
                    re = a_s[k, here, lanes] - b_s[k, low, lanes]
                    im = b_s[k, here, lanes] + a_s[k, low, lanes]
                else:
                    rim = slice(16 + 8 * band, 24 + 8 * band)
                    a, b = a_s[k, rim, lanes], b_s[k, rim, lanes]
                    re = a - pltpu.roll(b, 6, 0)
                    im = b + pltpu.roll(a, 6, 0)
                values.append(times((re, im), twist_ref[0, k : k + 1, lanes], twist_ref[1, k : k + 1, lanes]))
            for k, (re, im) in enumerate(sixteen(values)):
                spot = slice(256 * k + 128 * half, 256 * k + 128 * half + 128)
                if band < 2:
                    re_s[here, spot] = re
                    im_s[here, spot] = im
                power[here, spot] = re * re + im * im
    here = power[0:16]
    rim = power[16:32]
    row = lax.broadcasted_iota(jnp.int32, (16, NX), 0)
    lane = lax.broadcasted_iota(jnp.int32, (16, NX), 1)
    up = jnp.where((row & 3) == 0, rim, pltpu.roll(here, 1, 0))
    down = jnp.where((row & 3) == 3, pltpu.roll(rim, 2, 0), pltpu.roll(here, 15, 0))

    def moved(v, offset):
        if offset > 0:
            return jnp.where(lane < NX - offset, pltpu.roll(v, NX - offset, 1), 0.0)
        return jnp.where(lane >= -offset, pltpu.roll(v, -offset, 1), 0.0)

    row_small = lax.broadcasted_iota(jnp.int32, (16, 128), 0) >> 2

    def of_rows(which):
        value = jnp.zeros((16, 128), F32)
        for n in range(4):
            value = jnp.where(row_small == n, par_ref[which, pl.ds(8 * n + g, 1), :], value)
        return value[:, 0:1]

    depth, radius, gain = of_rows(0) * (1.0 / DEPTHS), of_rows(1), of_rows(2)
    vertical = up + 2.0 * here + down
    step = down - up
    across = moved(vertical, 1) - moved(vertical, -1)
    downward = moved(step, -1) + 2.0 * step + moved(step, 1)
    energy = across * across + downward * downward
    total = energy
    for offset in range(1, MAXWIDTH + 1):
        inside = (offset <= radius).astype(F32)
        total = total + inside * (moved(energy, -offset) + moved(energy, offset))
    smoothed = total / (2.0 * radius + 1.0)
    scores = gain * jnp.log(1.0 + smoothed)
    peak = jnp.maximum(scores[0:8], scores[8:16])
    peak = jnp.maximum(peak, pltpu.roll(peak, 4, 0))
    first, second = jnp.exp(scores[0:8] - peak), jnp.exp(scores[8:16] - peak)

    def joined(v):
        return (v + pltpu.roll(v, 4, 0))[0:4]

    records = (
        peak[0:4],
        joined(first + second),
        joined(first * depth[0:8] + second * depth[8:16]),
        joined(first * re_s[0:8] + second * re_s[8:16]),
        joined(first * im_s[0:8] + second * im_s[8:16]),
    )
    for n, record in enumerate(records):
        for target in range(32):
            out_ref[target, n] = record[:, 128 * target : 128 * target + 128]


def merge_kernel(in_ref, depth_ref, focus_ref):
    for q in range(4):
        spots = [4 * g + q for g in range(8)]
        peak = in_ref[spots[0], 0]
        for n in spots[1:]:
            peak = jnp.maximum(peak, in_ref[n, 0])
        weights = [jnp.exp(in_ref[n, 0] - peak) for n in spots]
        sums = [sum(w * in_ref[n, k] for w, n in zip(weights, spots)) for k in range(1, 5)]
        rows = slice(4 * q, 4 * q + 4)
        depth_ref[rows] = sums[1] / sums[0]
        focus_ref[0, rows] = sums[2] / sums[0]
        focus_ref[1, rows] = sums[3] / sums[0]


def params(mib):
    return pltpu.CompilerParams(vmem_limit_bytes=mib * 1024 * 1024)


def whole(shape):
    return pl.BlockSpec(shape, lambda *_: (0,) * len(shape))


def cost(flops, size):
    return pl.CostEstimate(flops=flops, bytes_accessed=size, transcendentals=0)


def shards(spectrum, plane_index, kernel_width, focus_gain):
    smem = pl.BlockSpec(memory_space=pltpu.SMEM)
    picked = pl.pallas_call(
        pick_kernel,
        in_specs=[smem, smem, smem, pl.BlockSpec(memory_space=pl.ANY)],
        out_specs=whole((32, 24, 128)),
        out_shape=jax.ShapeDtypeStruct((32, 24, 128), BF16),
        scratch_shapes=[pltpu.VMEM((2, 128, 256), BF16), pltpu.SemaphoreType.DMA(())],
        compiler_params=params(58),
        cost_estimate=cost(50_000_000, 300_000),
        name="pick",
    )(plane_index, kernel_width, focus_gain, spectrum)
    groups = [[16 * d + (d + j) % 16 for d in range(32)] for j in range(16)]
    columns = lax.all_to_all(
        picked, ALL, split_axis=0, concat_axis=0, tiled=True, axis_index_groups=groups
    )

    tables, row_table, twist = pl.pallas_call(
        table_kernel,
        grid=(BLOCKS,),
        in_specs=[],
        out_specs=[
            pl.BlockSpec((1, 2, PIECES, HALF, HALF), lambda b: (b, 0, 0, 0, 0)),
            whole((2, PIECES, HALF, HALF)),
            whole((2, 16, HALF)),
        ],
        out_shape=[
            jax.ShapeDtypeStruct((BLOCKS, 2, PIECES, HALF, HALF), BF16),
            jax.ShapeDtypeStruct((2, PIECES, HALF, HALF), BF16),
            jax.ShapeDtypeStruct((2, 16, HALF), F32),
        ],
        scratch_shapes=[pltpu.VMEM((HALF, HALF), F32), pltpu.VMEM((HALF, HALF), F32)],
        compiler_params=params(16),
        cost_estimate=cost(30_000_000, 5_000_000),
        name="tables",
    )()

    messages, planes = pl.pallas_call(
        column_kernel,
        grid=(BLOCKS,),
        in_specs=[
            whole((32, 24, 128)),
            pl.BlockSpec((1, 2, PIECES, HALF, HALF), lambda b: (b, 0, 0, 0, 0)),
        ],
        out_specs=[whole((1536, 128)), whole((3, 32, 128))],
        out_shape=[
            jax.ShapeDtypeStruct((1536, 128), F32),
            jax.ShapeDtypeStruct((3, 32, 128), F32),
        ],
        scratch_shapes=[
            pltpu.VMEM((2, HALF, HALF), F32),
            pltpu.VMEM((256, 128), F32),
            pltpu.VMEM((2, 64, 8, 128), F32),
        ],
        compiler_params=params(50),
        cost_estimate=cost(6_500_000_000, 8_000_000),
        name="columns",
    )(columns, tables)
    arrived = lax.all_to_all(
        messages.reshape(512, 1, 384), ALL, split_axis=0, concat_axis=0, tiled=True
    )

    records = pl.pallas_call(
        row_kernel,
        in_specs=[
            whole((1536, 128)),
            whole((3, 32, 128)),
            whole((2, PIECES, HALF, HALF)),
            whole((2, 16, HALF)),
        ],
        out_specs=whole((32, 5, 4, 128)),
        out_shape=jax.ShapeDtypeStruct((32, 5, 4, 128), F32),
        scratch_shapes=[
            pltpu.VMEM((16, 48, HALF), F32),
            pltpu.VMEM((16, 48, HALF), F32),
            pltpu.VMEM((16, 48, HALF), F32),
            pltpu.VMEM((32, NX), F32),
            pltpu.VMEM((16, NX), F32),
            pltpu.VMEM((16, NX), F32),
        ],
        compiler_params=params(24),
        cost_estimate=cost(1_000_000_000, 2_200_000),
        name="rows",
    )(arrived.reshape(1536, 128), planes, row_table, twist)
    merged = lax.all_to_all(records, "depth", split_axis=0, concat_axis=0, tiled=True)

    depth_map, focused = pl.pallas_call(
        merge_kernel,
        in_specs=[whole((32, 5, 4, 128))],
        out_specs=[whole((16, 128)), whole((2, 16, 128))],
        out_shape=[
            jax.ShapeDtypeStruct((16, 128), F32),
            jax.ShapeDtypeStruct((2, 16, 128), F32),
        ],
        compiler_params=params(4),
        cost_estimate=cost(1_000_000, 500_000),
        name="merge",
    )(merged)
    return depth_map, focused


def solution(mesh):
    return jax.shard_map(
        shards,
        mesh=mesh,
        in_specs=(P(None, "rows", None), P("depth"), P("depth"), P("depth")),
        out_specs=(P("rows", "depth"), P(None, "rows", "depth")),
        check_vma=False,
    )
```

time: 139 us -> 107 us (0.77)
  waiting for transfers between devices: 43.8 us -> 9.88 us
  blocking collectives: 26.7 us -> 54.6 us
  starting transfers between devices: 31.9 us -> 19.2 us
  Pallas kernels: 29.6 us -> 18.1 us
    all_to_all x0 -> x1, blocking collectives: none -> 38.1 us  [shards(): lax.all_to_all(messages.reshape(512, 1, 384), ALL, split_axis=0, concat_a...]
    all_to_all x4 -> x1, waiting for transfers between devices: 43.8 us -> 9.88 us  [shards(): lax.all_to_all(picked, ALL, split_axis=0, concat_axis=0, tiled=True, axis...]
    all_to_all x4 -> x1, starting transfers between devices: 31.9 us -> 19.2 us  [shards(): lax.all_to_all(picked, ALL, split_axis=0, concat_axis=0, tiled=True, axis...]
    all_to_all x1, blocking collectives: 26.7 us -> 16.5 us  [shards(): lax.all_to_all(records, 'depth', split_axis=0, concat_axis=0, tiled=True)]
    pallas_call x5 -> x4, Pallas kernels: 23.8 us -> 15.9 us  [the longest x1 9.66 us: shards(): pl.pallas_call(column_kernel, grid=(BLOCKS,), in_specs=[whole((32, 24, 12...]
    pallas_call x1, Pallas kernels: 5.8 us -> 2.18 us  [shards(): pl.pallas_call(table_kernel, grid=(BLOCKS,), in_specs=[], out_specs=[pl.B...]
  transfers between devices with their start and end apart: 4 -> 1, of which waited for: 4 -> 1; matrix products, arithmetic and copies ran while one was open for 1% -> 0% of each run, Pallas kernels for 6% -> 2%
where the time goes in v2:
time: 107 us; the launch traced here: 106 us
  blocking collectives  54.6 us (51%)
  starting transfers between devices  19.2 us (18%)
  Pallas kernels  18.1 us (17%)
  waiting for transfers between devices  9.88 us (9%)
  between operations  2.62 us (2%)
  local copies, waits for them, and re-layouts  1.93 us (2%)
    all_to_all x1, blocking collectives, shards(): lax.all_to_all(messages.reshape(512, 1, 384), ALL, split_axis=0, concat_a...  38.1 us
    all_to_all x1, starting transfers between devices, shards(): lax.all_to_all(picked, ALL, split_axis=0, concat_axis=0, tiled=True, axis...  19.2 us
    all_to_all x1, blocking collectives, shards(): lax.all_to_all(records, 'depth', split_axis=0, concat_axis=0, tiled=True)  16.5 us
    all_to_all x1, waiting for transfers between devices, shards(): lax.all_to_all(picked, ALL, split_axis=0, concat_axis=0, tiled=True, axis...  9.88 us
    pallas_call x1, Pallas kernels, shards(): pl.pallas_call(column_kernel, grid=(BLOCKS,), in_specs=[whole((32, 24, 12...  9.66 us
    pallas_call x1, Pallas kernels, shards(): pl.pallas_call(row_kernel, in_specs=[whole((1536, 128)), whole((3, 32, 12...  3.44 us
    pallas_call x1, Pallas kernels, shards(): pl.pallas_call(table_kernel, grid=(BLOCKS,), in_specs=[], out_specs=[pl.B...  2.18 us
  transfers between devices with their start and end apart: 1, of which 1 were waited for; matrix products, arithmetic and copies ran while one was open for 0% of the time, Pallas kernels for 2%

profile of v2, /device:TPU:1, one launch (start us, length us, event | category | flops | bytes accessed | tf_op | source)
XLA Modules:
  0.0 106.4 jit_solution(6816145426279063903)
XLA Ops:
  2.6 2.1 %pick.1 = bf16[32,24,128]{2,1,0:T(8,128)(2,1)} custom-call(s32[1]{0:T(128)S(6)} %copy.7.z_ref, s32[1]{0:T(128)S(6)} %copy.8.width_ref, f32[1]{0:T(128)S(6)} %copy.9.gain_ref, bf16[2,256,4096]{2,1,0:T(8,128)(2,1)} %spec_ref.1), custom_call_target="tpu_custom_call" | custom-call | flops 50000000 | bytes 300000 | tf_op jit(solution)/shard_map/pick/pallas_call | solution.py:404
  4.7 19.2 %all-to-all-start = ((bf16[32,24,128]{2,1,0:T(8,128)(2,1)}), bf16[32,24,128]{2,1,0:T(8,128)(2,1)S(1)}, u32[]{:S(2)}, u32[]{:S(2)}) async-start(bf16[32,24,128]{2,1,0:T(8,128)(2,1)} %pick.1), calls=%async_computation | async-start | bytes 393216 | tf_op jit(solution)/shard_map/all_to_all | solution.py:415
  23.9 2.2 %tables.1 = (bf16[8,2,2,256,256]{4,3,2,1,0:T(8,128)(2,1)S(1)}, bf16[2,2,256,256]{3,2,1,0:T(8,128)(2,1)S(1)}, f32[2,16,256]{2,1,0:T(8,128)S(1)}) custom-call(), custom_call_target="tpu_custom_call" | custom-call | flops 30000000 | bytes 5000000 | tf_op jit(solution)/shard_map/tables/pallas_call | solution.py:419
  26.1 0.0 copy-start
  26.1 1.9 %copy-done = bf16[8,2,2,256,256]{4,3,2,1,0:T(8,128)(2,1)} copy-done((bf16[8,2,2,256,256]{4,3,2,1,0:T(8,128)(2,1)}, bf16[8,2,2,256,256]{4,3,2,1,0:T(8,128)(2,1)S(1)}, u32[]{:S(2)}) %copy-start) | copy-done | bytes 4194328
  28.1 9.9 %all-to-all-done.spec_ref = bf16[32,24,128]{2,1,0:T(8,128)(2,1)S(1)} async-done(((bf16[32,24,128]{2,1,0:T(8,128)(2,1)}), bf16[32,24,128]{2,1,0:T(8,128)(2,1)S(1)}, u32[]{:S(2)}, u32[]{:S(2)}) %all-to-all-start) | async-done | bytes 196640 | tf_op jit(solution)/shard_map/all_to_all | solution.py:415
  37.9 9.7 %columns.1 = (f32[1536,128]{1,0:T(8,128)S(1)}, f32[3,32,128]{2,1,0:T(8,128)S(1)}) custom-call(bf16[32,24,128]{2,1,0:T(8,128)(2,1)S(1)} %all-to-all-done.spec_ref, bf16[8,2,2,256,256]{4,3,2,1,0:T(8,128)(2,1)} %copy-done), custom_call_target="tpu_custom_call" | custom-call | flops 6499999744 | bytes 8000000 | tf_op jit(solution)/shard_map/columns/pallas_call | solution.py:439
  47.6 38.1 %all_to_all.15 = f32[512,1,384]{2,1,0:T(1,128)S(1)} all-to-all(f32[512,1,384]{2,1,0:T(1,128)S(1)} %bitcast.3), channel_id=1, replica_groups=mesh['depth'=32,'rows'=16] {'depth','rows'}, dimensions={0} | all-to-all | bytes 1572864 | tf_op jit(solution)/shard_map/all_to_all | solution.py:460
  85.8 3.4 %rows.1 = f32[32,5,4,128]{3,2,1,0:T(4,128)S(1)} custom-call(f32[1536,128]{1,0:T(8,128)S(1)} %bitcast.2, f32[3,32,128]{2,1,0:T(8,128)S(1)} %get-tuple-element.9.par_ref, bf16[2,2,256,256]{3,2,1,0:T(8,128)(2,1)S(1)} %get-tuple-element.10.row_ref, f32[2,16,256]{2,1,0:T(8,128)S(1)} %get-tuple-element.11.twist_ref), custom_call_target="tpu_custom_call" | custom-call | flops 1000000000 | bytes 2200000 | tf_op jit(solution)/shard_map/rows/pallas_call | solution.py:464
  89.2 16.5 %all_to_all.16.in_ref = f32[32,5,4,128]{3,2,1,0:T(4,128)S(1)} all-to-all(f32[32,5,4,128]{3,2,1,0:T(4,128)S(1)} %rows.1), channel_id=1, replica_groups=mesh['depth'=32,'rows'=16] {'depth'}, dimensions={0} | all-to-all | bytes 655360 | tf_op jit(solution)/shard_map/all_to_all | solution.py:486
  105.7 0.7 merge.1
Async XLA Ops:
  4.7 33.3 %all-to-all-start = ((bf16[32,24,128]{2,1,0:T(8,128)(2,1)}), bf16[32,24,128]{2,1,0:T(8,128)(2,1)S(1)}, u32[]{:S(2)}, u32[]{:S(2)}) async-start(bf16[32,24,128]{2,1,0:T(8,128)(2,1)} %pick.1), calls=%async_computation | async-start | bytes 393216 | tf_op jit(solution)/shard_map/all_to_all | solution.py:415
  26.1 1.9 %copy-start = (bf16[8,2,2,256,256]{4,3,2,1,0:T(8,128)(2,1)}, bf16[8,2,2,256,256]{4,3,2,1,0:T(8,128)(2,1)S(1)}, u32[]{:S(2)}) copy-start(bf16[8,2,2,256,256]{4,3,2,1,0:T(8,128)(2,1)S(1)} %get-tuple-element.7.tab_ref) | copy-start | bytes 12582916

commit v3 on v2

--- a/solution.py
+++ b/solution.py
@@ -82,6 +82,32 @@
                 parts[i + step] = jnp.where(low, pltpu.roll(x, 128 - group * step, 1), y)
         step *= 2
     return parts
+
+
+def packed(re, im, rim):
+    most = jnp.maximum(jnp.maximum(jnp.abs(re), jnp.abs(im)), jnp.abs(rim))
+    small = most < 2.0**-40
+    lift = jnp.where(small, 2.0**80, 1.0)
+    power = jnp.floor(jnp.log2(jnp.maximum(most * lift, 2.0**-46)) + 0.01).astype(jnp.int32) + 1
+    scale = jnp.exp2((18 - power).astype(F32)) * lift
+
+    def whole_number(v):
+        return jnp.floor(v + 0.5).astype(jnp.int32)
+
+    a, b, c = whole_number(re * scale), whole_number(im * scale), whole_number(rim * scale * 0.5)
+    code = power + jnp.where(small, 128 - 80, 128)
+    first = (a << 13) | (code << 5) | (c & 31)
+    second = (b << 13) | ((c >> 5) & 0x1FFF)
+    return first, second
+
+
+def unpacked(first, second):
+    power = ((first >> 5) & 255) - 128
+    small = power < -40
+    scale = jnp.exp2((jnp.where(small, power + 80, power) - 18).astype(F32))
+    scale = scale * jnp.where(small, 2.0**-80, 1.0)
+    c = (((second << 19) >> 19) << 5) + (first & 31)
+    return (first >> 13).astype(F32) * scale, (second >> 13).astype(F32) * scale, c.astype(F32) * (scale * 2.0)
 
 
 def pick_kernel(z_ref, width_ref, gain_ref, spec_ref, out_ref, buf, sem):
@@ -241,10 +267,10 @@
                 jnp.where(slot == 0, pltpu.roll(above[0], 125, 1), pltpu.roll(below[0], 1, 1)),
                 jnp.where(slot == 2, pltpu.roll(above[1], 127, 1), pltpu.roll(below[1], 3, 1)),
             )
-            item = 3 * ((n & 3) * 16 + (n >> 2))
-            out_ref[pl.ds(item, 8, stride=192), :] = bands[0, n]
-            out_ref[pl.ds(item + 1, 8, stride=192), :] = bands[1, n]
-            out_ref[pl.ds(item + 2, 8, stride=192), :] = rim
+            item = 2 * ((n & 3) * 16 + (n >> 2))
+            first, second = packed(bands[0, n], bands[1, n], rim)
+            out_ref[pl.ds(item, 8, stride=128), :] = first
+            out_ref[pl.ds(item + 1, 8, stride=128), :] = second
 
 
 def times_i(v):
@@ -286,13 +312,15 @@
     d, _, _ = places()
     g = d >> 2
     for quad in range(4):
+        rows = [[], [], []]
+        for n in range(4):
+            for half in range(2):
+                start = 32 * (4 * quad + n + 16 * half)
+                words = [in_ref[pl.ds(start + m, 16, stride=2), :] for m in range(2)]
+                for piece, value in enumerate(unpacked(*words)):
+                    rows[piece].append(value)
         for piece in range(3):
-            rows = []
-            for n in range(4):
-                for half in range(2):
-                    start = 48 * (4 * quad + n + 16 * half) + piece
-                    rows.append(in_ref[pl.ds(start, 16, stride=3), :])
-            turned = jnp.concatenate(rows, axis=0).T
+            turned = jnp.concatenate(rows[piece], axis=0).T
             for a in range(2):
                 parts = swapped([turned[64 * a + 16 * n : 64 * a + 16 * n + 16] for n in range(4)], 32)
                 for n, part in enumerate(parts):
@@ -443,9 +471,9 @@
             whole((32, 24, 128)),
             pl.BlockSpec((1, 2, PIECES, HALF, HALF), lambda b: (b, 0, 0, 0, 0)),
         ],
-        out_specs=[whole((1536, 128)), whole((3, 32, 128))],
+        out_specs=[whole((1024, 128)), whole((3, 32, 128))],
         out_shape=[
-            jax.ShapeDtypeStruct((1536, 128), F32),
+            jax.ShapeDtypeStruct((1024, 128), jnp.int32),
             jax.ShapeDtypeStruct((3, 32, 128), F32),
         ],
         scratch_shapes=[
@@ -458,13 +486,13 @@
         name="columns",
     )(columns, tables)
     arrived = lax.all_to_all(
-        messages.reshape(512, 1, 384), ALL, split_axis=0, concat_axis=0, tiled=True
+        messages.reshape(512, 1, 256), ALL, split_axis=0, concat_axis=0, tiled=True
     )
 
     records = pl.pallas_call(
         row_kernel,
         in_specs=[
-            whole((1536, 128)),
+            whole((1024, 128)),
             whole((3, 32, 128)),
             whole((2, PIECES, HALF, HALF)),
             whole((2, 16, HALF)),
@@ -482,7 +510,7 @@
         compiler_params=params(24),
         cost_estimate=cost(1_000_000_000, 2_200_000),
         name="rows",
-    )(arrived.reshape(1536, 128), planes, row_table, twist)
+    )(arrived.reshape(1024, 128), planes, row_table, twist)
     merged = lax.all_to_all(records, "depth", split_axis=0, concat_axis=0, tiled=True)
 
     depth_map, focused = pl.pallas_call(

time: 107 us -> 102 us (0.953)
  blocking collectives: 54.6 us -> 49 us
    all_to_all x1, blocking collectives: 38.1 us -> 32.6 us  [shards(): lax.all_to_all(messages.reshape(512, 1, 256), ALL, split_axis=0, concat_a...]
where the time goes in v3:
time: 102 us; the launch traced here: 101 us
  blocking collectives  49 us (48%)
  starting transfers between devices  19.2 us (19%)
  Pallas kernels  18.2 us (18%)
  waiting for transfers between devices  9.88 us (10%)
  between operations  2.62 us (3%)
  local copies, waits for them, and re-layouts  1.93 us (2%)
    all_to_all x1, blocking collectives, shards(): lax.all_to_all(messages.reshape(512, 1, 256), ALL, split_axis=0, concat_a...  32.6 us
    all_to_all x1, starting transfers between devices, shards(): lax.all_to_all(picked, ALL, split_axis=0, concat_axis=0, tiled=True, axis...  19.2 us
    all_to_all x1, blocking collectives, shards(): lax.all_to_all(records, 'depth', split_axis=0, concat_axis=0, tiled=True)  16.4 us
    all_to_all x1, waiting for transfers between devices, shards(): lax.all_to_all(picked, ALL, split_axis=0, concat_axis=0, tiled=True, axis...  9.88 us
    pallas_call x1, Pallas kernels, shards(): pl.pallas_call(column_kernel, grid=(BLOCKS,), in_specs=[whole((32, 24, 12...  9.77 us
    pallas_call x1, Pallas kernels, shards(): pl.pallas_call(row_kernel, in_specs=[whole((1024, 128)), whole((3, 32, 12...  3.46 us
    pallas_call x1, Pallas kernels, shards(): pl.pallas_call(table_kernel, grid=(BLOCKS,), in_specs=[], out_specs=[pl.B...  2.18 us
    pallas_call x1, Pallas kernels, shards(): pl.pallas_call(pick_kernel, in_specs=[smem, smem, smem, pl.BlockSpec(memo...  2.11 us
  transfers between devices with their start and end apart: 1, of which 1 were waited for; matrix products, arithmetic and copies ran while one was open for 0% of the time, Pallas kernels for 2%

profile of v3, /device:TPU:1, one launch (start us, length us, event | category | flops | bytes accessed | tf_op | source)
XLA Modules:
  0.0 100.9 jit_solution(13014637871387183851)
XLA Ops:
  2.6 2.1 %pick.1 = bf16[32,24,128]{2,1,0:T(8,128)(2,1)} custom-call(s32[1]{0:T(128)S(6)} %copy.7.z_ref, s32[1]{0:T(128)S(6)} %copy.8.width_ref, f32[1]{0:T(128)S(6)} %copy.9.gain_ref, bf16[2,256,4096]{2,1,0:T(8,128)(2,1)} %spec_ref.1), custom_call_target="tpu_custom_call" | custom-call | flops 50000000 | bytes 300000 | tf_op jit(solution)/shard_map/pick/pallas_call | solution.py:432
  4.7 19.2 %all-to-all-start = ((bf16[32,24,128]{2,1,0:T(8,128)(2,1)}), bf16[32,24,128]{2,1,0:T(8,128)(2,1)S(1)}, u32[]{:S(2)}, u32[]{:S(2)}) async-start(bf16[32,24,128]{2,1,0:T(8,128)(2,1)} %pick.1), calls=%async_computation | async-start | bytes 393216 | tf_op jit(solution)/shard_map/all_to_all | solution.py:443
  23.9 2.2 %tables.1 = (bf16[8,2,2,256,256]{4,3,2,1,0:T(8,128)(2,1)S(1)}, bf16[2,2,256,256]{3,2,1,0:T(8,128)(2,1)S(1)}, f32[2,16,256]{2,1,0:T(8,128)S(1)}) custom-call(), custom_call_target="tpu_custom_call" | custom-call | flops 30000000 | bytes 5000000 | tf_op jit(solution)/shard_map/tables/pallas_call | solution.py:447
  26.1 0.0 copy-start
  26.1 1.9 %copy-done = bf16[8,2,2,256,256]{4,3,2,1,0:T(8,128)(2,1)} copy-done((bf16[8,2,2,256,256]{4,3,2,1,0:T(8,128)(2,1)}, bf16[8,2,2,256,256]{4,3,2,1,0:T(8,128)(2,1)S(1)}, u32[]{:S(2)}) %copy-start) | copy-done | bytes 4194328
  28.1 9.9 %all-to-all-done.spec_ref = bf16[32,24,128]{2,1,0:T(8,128)(2,1)S(1)} async-done(((bf16[32,24,128]{2,1,0:T(8,128)(2,1)}), bf16[32,24,128]{2,1,0:T(8,128)(2,1)S(1)}, u32[]{:S(2)}, u32[]{:S(2)}) %all-to-all-start) | async-done | bytes 196640 | tf_op jit(solution)/shard_map/all_to_all | solution.py:443
  37.9 9.8 %columns.1 = (s32[1024,128]{1,0:T(8,128)S(1)}, f32[3,32,128]{2,1,0:T(8,128)S(1)}) custom-call(bf16[32,24,128]{2,1,0:T(8,128)(2,1)S(1)} %all-to-all-done.spec_ref, bf16[8,2,2,256,256]{4,3,2,1,0:T(8,128)(2,1)} %copy-done), custom_call_target="tpu_custom_call" | custom-call | flops 6499999744 | bytes 8000000 | tf_op jit(solution)/shard_map/columns/pallas_call | solution.py:467
  47.7 32.6 %all_to_all.15 = s32[512,1,256]{2,1,0:T(1,128)S(1)} all-to-all(s32[512,1,256]{2,1,0:T(1,128)S(1)} %bitcast.3), channel_id=1, replica_groups=mesh['depth'=32,'rows'=16] {'depth','rows'}, dimensions={0} | all-to-all | bytes 1048576 | tf_op jit(solution)/shard_map/all_to_all | solution.py:488
  80.3 3.5 %rows.1 = f32[32,5,4,128]{3,2,1,0:T(4,128)S(1)} custom-call(s32[1024,128]{1,0:T(8,128)S(1)} %bitcast.2, f32[3,32,128]{2,1,0:T(8,128)S(1)} %get-tuple-element.9.par_ref, bf16[2,2,256,256]{3,2,1,0:T(8,128)(2,1)S(1)} %get-tuple-element.10.row_ref, f32[2,16,256]{2,1,0:T(8,128)S(1)} %get-tuple-element.11.twist_ref), custom_call_target="tpu_custom_call" | custom-call | flops 1000000000 | bytes 2200000 | tf_op jit(solution)/shard_map/rows/pallas_call | solution.py:492
  83.8 16.4 %all_to_all.16.in_ref = f32[32,5,4,128]{3,2,1,0:T(4,128)S(1)} all-to-all(f32[32,5,4,128]{3,2,1,0:T(4,128)S(1)} %rows.1), channel_id=1, replica_groups=mesh['depth'=32,'rows'=16] {'depth'}, dimensions={0} | all-to-all | bytes 655360 | tf_op jit(solution)/shard_map/all_to_all | solution.py:514
  100.2 0.7 merge.1
Async XLA Ops:
  4.7 33.3 %all-to-all-start = ((bf16[32,24,128]{2,1,0:T(8,128)(2,1)}), bf16[32,24,128]{2,1,0:T(8,128)(2,1)S(1)}, u32[]{:S(2)}, u32[]{:S(2)}) async-start(bf16[32,24,128]{2,1,0:T(8,128)(2,1)} %pick.1), calls=%async_computation | async-start | bytes 393216 | tf_op jit(solution)/shard_map/all_to_all | solution.py:443
  26.1 1.9 %copy-start = (bf16[8,2,2,256,256]{4,3,2,1,0:T(8,128)(2,1)}, bf16[8,2,2,256,256]{4,3,2,1,0:T(8,128)(2,1)S(1)}, u32[]{:S(2)}) copy-start(bf16[8,2,2,256,256]{4,3,2,1,0:T(8,128)(2,1)S(1)} %get-tuple-element.7.tab_ref) | copy-start | bytes 12582916

commit v4 on v3

--- a/solution.py
+++ b/solution.py
@@ -144,7 +144,7 @@
     out_ref[...] = jnp.concatenate(both, axis=1).astype(BF16)
 
 
-def table_kernel(tab_ref, row_ref, twist_ref, base_c, base_s):
+def table_kernel(high_ref, low_ref, row_ref, twist_ref, base_c, base_s):
     b = pl.program_id(0)
     l = lax.broadcasted_iota(jnp.int32, (HALF, HALF), 0)
     y = lax.broadcasted_iota(jnp.int32, (HALF, HALF), 1)
@@ -173,104 +173,99 @@
     sine = base_s[...] * c16 + base_c[...] * s16
     nyquist = (1 - 2 * (y & 1)).astype(F32)
     sine = jnp.where((l == 0) & (b == 0), nyquist, sine)
-    for n, part in enumerate(pieces(cosine)):
-        tab_ref[0, 0, n] = part
-    for n, part in enumerate(pieces(sine)):
-        tab_ref[0, 1, n] = part
-
-
-def column_kernel(spec_ref, tab_ref, out_ref, par_ref, acc, par_s, bands):
-    b = pl.program_id(0)
+    for t, value in enumerate((cosine, sine)):
+        high_ref[0, t], low_ref[0, t] = pieces(value)
+
+
+def column_kernel(spec_ref, high_ref, low_hbm, out_ref, par_ref, acc, par_s, bands, low_s, sems):
     d, r, j = places()
 
-    @pl.when(b == 0)
-    def _():
-        par_s[...] = spec_ref[:, 16:24].astype(F32).reshape(256, 128)
-        rows = [par_s[pl.ds(n, 32, stride=8), :] for n in range(6)]
-        par_ref[0] = rows[0] + rows[1]
-        par_ref[1] = rows[2]
-        par_ref[2] = rows[3] + rows[4] + rows[5]
-
-    lane = lax.broadcasted_iota(jnp.int32, (32, HALF), 1)
-    special = (lane == 0) & (b == 0)
+    def fetch(n):
+        return pltpu.make_async_copy(low_hbm.at[n], low_s.at[n], sems.at[n])
+
+    for n in range(BLOCKS):
+        fetch(n).start()
+    par_s[...] = spec_ref[:, 16:24].astype(F32).reshape(256, 128)
+    rows = [par_s[pl.ds(n, 32, stride=8), :] for n in range(6)]
+    par_ref[0] = rows[0] + rows[1]
+    par_ref[1] = rows[2]
+    par_ref[2] = rows[3] + rows[4] + rows[5]
     z = par_ref[0].astype(jnp.int32)
-    z2 = jnp.concatenate([z, z], axis=1)
-    s = jnp.where(special, NX // 2, b * HALF + lane)
-    c_o, s_o = cos_sin(chirp_turns(z2, s))
-    s_o = -s_o
-    c_e = jnp.where(special, 1.0, c_o)
-    s_e = jnp.where(special, 0.0, s_o)
-
-    def block(n):
-        return spec_ref[(((n >> 1) - j) & 15) + 16 * (n & 1), 0:16].astype(F32)
-
-    lane16 = lax.broadcasted_iota(jnp.int32, (16, HALF), 1)
-    plus = jnp.concatenate([block(2 * b), block(2 * b + 1)], axis=1)
-    middle = block(31 - 2 * b)
-    last = jnp.concatenate([middle, block(30 - 2 * b)], axis=1)
-    first = jnp.concatenate([block(jnp.where(b == 0, 16, 32 - 2 * b)), middle], axis=1)
-    minus = jnp.where((lane16 & 127) == 0, first, last)
-    corner = (lane16 == 0) & (b == 0)
-    even = jnp.where(corner, plus, plus + minus)
-    odd = plus - minus
-    o_re = jnp.where(corner[:8], minus[:8], -odd[8:])
-    o_im = jnp.where(corner[:8], minus[8:], odd[:8])
-    e_re, e_im = even[:8], even[8:]
-
-    def turned(re, im, c, s):
-        re, im = re[:, None, :], im[:, None, :]
-        t_re = (re * c[None] - im * s[None]).reshape(HALF, HALF)
-        t_im = (re * s[None] + im * c[None]).reshape(HALF, HALF)
-        return t_re, t_im
-
-    parts = []
-    for t, (re, im, c, s) in enumerate(((e_re, e_im, c_e, s_e), (o_re, o_im, c_o, s_o))):
-        for value in turned(re, im, c, s):
-            parts.append(product(pieces(value), [tab_ref[0, t, n] for n in range(PIECES)]))
+    acc[...] = jnp.zeros_like(acc)
+
+    def step(b, carry):
+        fetch(b).wait()
+        lane = lax.broadcasted_iota(jnp.int32, (32, HALF), 1)
+        special = (lane == 0) & (b == 0)
+        z2 = jnp.concatenate([z, z], axis=1)
+        s = jnp.where(special, NX // 2, b * HALF + lane)
+        c_o, s_o = cos_sin(chirp_turns(z2, s))
+        s_o = -s_o
+        c_e = jnp.where(special, 1.0, c_o)
+        s_e = jnp.where(special, 0.0, s_o)
+
+        def block(n):
+            return spec_ref[(((n >> 1) - j) & 15) + 16 * (n & 1), 0:16].astype(F32)
+
+        lane16 = lax.broadcasted_iota(jnp.int32, (16, HALF), 1)
+        plus = jnp.concatenate([block(2 * b), block(2 * b + 1)], axis=1)
+        middle = block(31 - 2 * b)
+        last = jnp.concatenate([middle, block(30 - 2 * b)], axis=1)
+        first = jnp.concatenate([block(jnp.where(b == 0, 16, 32 - 2 * b)), middle], axis=1)
+        minus = jnp.where((lane16 & 127) == 0, first, last)
+        corner = (lane16 == 0) & (b == 0)
+        even = jnp.where(corner, plus, plus + minus)
+        odd = plus - minus
+        o_re = jnp.where(corner[:8], minus[:8], -odd[8:])
+        o_im = jnp.where(corner[:8], minus[8:], odd[:8])
+        e_re, e_im = even[:8], even[8:]
+
+        def turned(re, im, c, s):
+            re, im = re[:, None, :], im[:, None, :]
+            t_re = (re * c[None] - im * s[None]).reshape(HALF, HALF)
+            t_im = (re * s[None] + im * c[None]).reshape(HALF, HALF)
+            return t_re, t_im
+
+        parts = []
+        for t, (re, im, c, s) in enumerate(((e_re, e_im, c_e, s_e), (o_re, o_im, c_o, s_o))):
+            for value in turned(re, im, c, s):
+                parts.append(product(pieces(value), [high_ref[b, t], low_s[b, t]]))
+        for half in range(2):
+            acc[half] += parts[half] + parts[half + 2]
+        return carry
+
+    lax.fori_loop(0, BLOCKS, step, 0, unroll=4)
+    lane = lax.broadcasted_iota(jnp.int32, (8, 128), 1)
+    group = (lane >> 2) & 3
+    plane = z[0:8]
+    for n in range(1, 4):
+        plane = jnp.where(group == n, z[8 * n : 8 * n + 8], plane)
+    v = 256 * j + 128 * (d >> 4) + 16 * (lane >> 4) + (d & 15)
+    c, s = cos_sin(chirp_turns(plane, jnp.where(v < NX // 2, v, v - NX)))
+    s = -s
     for half in range(2):
-        total = parts[half] + parts[half + 2]
-
-        @pl.when(b == 0)
-        def _():
-            acc[half] = total
-
-        @pl.when(b > 0)
-        def _():
-            acc[half] = acc[half] + total
-
-    @pl.when(b == BLOCKS - 1)
-    def _():
-        lane = lax.broadcasted_iota(jnp.int32, (8, 128), 1)
-        group = (lane >> 2) & 3
-        plane = z[0:8]
-        for n in range(1, 4):
-            plane = jnp.where(group == n, z[8 * n : 8 * n + 8], plane)
-        v = 256 * j + 128 * (d >> 4) + 16 * (lane >> 4) + (d & 15)
-        c, s = cos_sin(chirp_turns(plane, jnp.where(v < NX // 2, v, v - NX)))
-        s = -s
-        for half in range(2):
-            cols = slice(128 * half, 128 * half + 128)
-            for part in range(2):
-                for n, v in enumerate(swapped([acc[part, 8 * i : 8 * i + 8, cols] for i in range(32)], 4)):
-                    bands[part, 32 * half + n] = v
-        for n in range(64):
-            re, im = bands[0, n], bands[1, n]
-            bands[0, n] = re * c - im * s
-            bands[1, n] = re * s + im * c
-        slot = lane & 3
-        for n in range(64):
-            zero = jnp.zeros((8, 128), F32)
-            above = [bands[part, n - 1] if n > 0 else zero for part in range(2)]
-            below = [bands[part, n + 1] if n < 63 else zero for part in range(2)]
-            rim = jnp.where(
-                slot < 2,
-                jnp.where(slot == 0, pltpu.roll(above[0], 125, 1), pltpu.roll(below[0], 1, 1)),
-                jnp.where(slot == 2, pltpu.roll(above[1], 127, 1), pltpu.roll(below[1], 3, 1)),
-            )
-            item = 2 * ((n & 3) * 16 + (n >> 2))
-            first, second = packed(bands[0, n], bands[1, n], rim)
-            out_ref[pl.ds(item, 8, stride=128), :] = first
-            out_ref[pl.ds(item + 1, 8, stride=128), :] = second
+        cols = slice(128 * half, 128 * half + 128)
+        for part in range(2):
+            for n, v in enumerate(swapped([acc[part, 8 * i : 8 * i + 8, cols] for i in range(32)], 4)):
+                bands[part, 32 * half + n] = v
+    for n in range(64):
+        re, im = bands[0, n], bands[1, n]
+        bands[0, n] = re * c - im * s
+        bands[1, n] = re * s + im * c
+    slot = lane & 3
+    for n in range(64):
+        zero = jnp.zeros((8, 128), F32)
+        above = [bands[part, n - 1] if n > 0 else zero for part in range(2)]
+        below = [bands[part, n + 1] if n < 63 else zero for part in range(2)]
+        rim = jnp.where(
+            slot < 2,
+            jnp.where(slot == 0, pltpu.roll(above[0], 125, 1), pltpu.roll(below[0], 1, 1)),
+            jnp.where(slot == 2, pltpu.roll(above[1], 127, 1), pltpu.roll(below[1], 3, 1)),
+        )
+        item = 2 * ((n & 3) * 16 + (n >> 2))
+        first, second = packed(bands[0, n], bands[1, n], rim)
+        out_ref[pl.ds(item, 8, stride=128), :] = first
+        out_ref[pl.ds(item + 1, 8, stride=128), :] = second
 
 
 def times_i(v):
@@ -444,17 +439,19 @@
         picked, ALL, split_axis=0, concat_axis=0, tiled=True, axis_index_groups=groups
     )
 
-    tables, row_table, twist = pl.pallas_call(
+    high, low, row_table, twist = pl.pallas_call(
         table_kernel,
         grid=(BLOCKS,),
         in_specs=[],
         out_specs=[
-            pl.BlockSpec((1, 2, PIECES, HALF, HALF), lambda b: (b, 0, 0, 0, 0)),
+            pl.BlockSpec((1, 2, HALF, HALF), lambda b: (b, 0, 0, 0)),
+            pl.BlockSpec((1, 2, HALF, HALF), lambda b: (b, 0, 0, 0)),
             whole((2, PIECES, HALF, HALF)),
             whole((2, 16, HALF)),
         ],
         out_shape=[
-            jax.ShapeDtypeStruct((BLOCKS, 2, PIECES, HALF, HALF), BF16),
+            jax.ShapeDtypeStruct((BLOCKS, 2, HALF, HALF), BF16),
+            jax.ShapeDtypeStruct((BLOCKS, 2, HALF, HALF), BF16),
             jax.ShapeDtypeStruct((2, PIECES, HALF, HALF), BF16),
             jax.ShapeDtypeStruct((2, 16, HALF), F32),
         ],
@@ -466,10 +463,10 @@
 
     messages, planes = pl.pallas_call(
         column_kernel,
-        grid=(BLOCKS,),
         in_specs=[
             whole((32, 24, 128)),
-            pl.BlockSpec((1, 2, PIECES, HALF, HALF), lambda b: (b, 0, 0, 0, 0)),
+            whole((BLOCKS, 2, HALF, HALF)),
+            pl.BlockSpec(memory_space=pl.ANY),
         ],
         out_specs=[whole((1024, 128)), whole((3, 32, 128))],
         out_shape=[
@@ -480,11 +477,13 @@
             pltpu.VMEM((2, HALF, HALF), F32),
             pltpu.VMEM((256, 128), F32),
             pltpu.VMEM((2, 64, 8, 128), F32),
+            pltpu.VMEM((BLOCKS, 2, HALF, HALF), BF16),
+            pltpu.SemaphoreType.DMA((BLOCKS,)),
         ],
         compiler_params=params(50),
         cost_estimate=cost(6_500_000_000, 8_000_000),
         name="columns",
-    )(columns, tables)
+    )(columns, high, low)
     arrived = lax.all_to_all(
         messages.reshape(512, 1, 256), ALL, split_axis=0, concat_axis=0, tiled=True
     )

time: 102 us -> 99.3 us (0.974)
  Pallas kernels: 18.2 us -> 15.8 us
    pallas_call x1, Pallas kernels: 9.77 us -> 7.37 us  [shards(): pl.pallas_call(column_kernel, in_specs=[whole((32, 24, 128)), whole((BLOC...]
where the time goes in v4:
time: 99.3 us; the launch traced here: 98.5 us
  blocking collectives  49 us (49%)
  starting transfers between devices  19.2 us (19%)
  Pallas kernels  15.8 us (16%)
  waiting for transfers between devices  10.5 us (11%)
  between operations  2.62 us (3%)
  local copies, waits for them, and re-layouts  1.32 us (1%)
    all_to_all x1, blocking collectives, shards(): lax.all_to_all(messages.reshape(512, 1, 256), ALL, split_axis=0, concat_a...  32.6 us
    all_to_all x1, starting transfers between devices, shards(): lax.all_to_all(picked, ALL, split_axis=0, concat_axis=0, tiled=True, axis...  19.2 us
    all_to_all x1, blocking collectives, shards(): lax.all_to_all(records, 'depth', split_axis=0, concat_axis=0, tiled=True)  16.4 us
    all_to_all x1, waiting for transfers between devices, shards(): lax.all_to_all(picked, ALL, split_axis=0, concat_axis=0, tiled=True, axis...  10.5 us
    pallas_call x1, Pallas kernels, shards(): pl.pallas_call(column_kernel, in_specs=[whole((32, 24, 128)), whole((BLOC...  7.37 us
    pallas_call x1, Pallas kernels, shards(): pl.pallas_call(row_kernel, in_specs=[whole((1024, 128)), whole((3, 32, 12...  3.46 us
    pallas_call x1, Pallas kernels, shards(): pl.pallas_call(table_kernel, grid=(BLOCKS,), in_specs=[], out_specs=[pl.B...  2.18 us
    pallas_call x1, Pallas kernels, shards(): pl.pallas_call(pick_kernel, in_specs=[smem, smem, smem, pl.BlockSpec(memo...  2.13 us
  transfers between devices with their start and end apart: 1, of which 1 were waited for; matrix products, arithmetic and copies ran while one was open for 0% of the time, Pallas kernels for 2%

profile of v4, /device:TPU:1, one launch (start us, length us, event | category | flops | bytes accessed | tf_op | source)
XLA Modules:
  0.0 98.5 jit_solution(12337404972794514447)
XLA Ops:
  2.6 2.1 %pick.1 = bf16[32,24,128]{2,1,0:T(8,128)(2,1)} custom-call(s32[1]{0:T(128)S(6)} %copy.7.z_ref, s32[1]{0:T(128)S(6)} %copy.8.width_ref, f32[1]{0:T(128)S(6)} %copy.9.gain_ref, bf16[2,256,4096]{2,1,0:T(8,128)(2,1)} %spec_ref.1), custom_call_target="tpu_custom_call" | custom-call | flops 50000000 | bytes 300000 | tf_op jit(solution)/shard_map/pick/pallas_call | solution.py:427
  4.7 19.2 %all-to-all-start = ((bf16[32,24,128]{2,1,0:T(8,128)(2,1)}), bf16[32,24,128]{2,1,0:T(8,128)(2,1)S(1)}, u32[]{:S(2)}, u32[]{:S(2)}) async-start(bf16[32,24,128]{2,1,0:T(8,128)(2,1)} %pick.1), calls=%async_computation | async-start | bytes 393216 | tf_op jit(solution)/shard_map/all_to_all | solution.py:438
  24.0 2.2 %tables.1 = (bf16[8,2,256,256]{3,2,1,0:T(8,128)(2,1)S(1)}, bf16[8,2,256,256]{3,2,1,0:T(8,128)(2,1)S(1)}, bf16[2,2,256,256]{3,2,1,0:T(8,128)(2,1)S(1)}, f32[2,16,256]{2,1,0:T(8,128)S(1)}) custom-call(), custom_call_target="tpu_custom_call" | custom-call | flops 30000000 | bytes 5000000 | tf_op jit(solution)/shard_map/tables/pallas_call | solution.py:442
  26.1 0.0 copy-start
  26.2 1.3 %copy-done = bf16[8,2,256,256]{3,2,1,0:T(8,128)(2,1)} copy-done((bf16[8,2,256,256]{3,2,1,0:T(8,128)(2,1)}, bf16[8,2,256,256]{3,2,1,0:T(8,128)(2,1)S(1)}, u32[]{:S(2)}) %copy-start) | copy-done | bytes 2097176
  27.5 10.5 %all-to-all-done.spec_ref = bf16[32,24,128]{2,1,0:T(8,128)(2,1)S(1)} async-done(((bf16[32,24,128]{2,1,0:T(8,128)(2,1)}), bf16[32,24,128]{2,1,0:T(8,128)(2,1)S(1)}, u32[]{:S(2)}, u32[]{:S(2)}) %all-to-all-start) | async-done | bytes 196640 | tf_op jit(solution)/shard_map/all_to_all | solution.py:438
  38.0 7.4 %columns.1 = (s32[1024,128]{1,0:T(8,128)S(1)}, f32[3,32,128]{2,1,0:T(8,128)S(1)}) custom-call(bf16[32,24,128]{2,1,0:T(8,128)(2,1)S(1)} %all-to-all-done.spec_ref, bf16[8,2,256,256]{3,2,1,0:T(8,128)(2,1)S(1)} %get-tuple-element.8.high_ref, bf16[8,2,256,256]{3,2,1,0:T(8,128)(2,1)} %copy-done), custom_call_target="tpu_custom_call" | custom-call | flops 6499999744 | bytes 8000000 | tf_op jit(solution)/shard_map/columns/pallas_call | solution.py:464
  45.4 32.6 %all_to_all.15 = s32[512,1,256]{2,1,0:T(1,128)S(1)} all-to-all(s32[512,1,256]{2,1,0:T(1,128)S(1)} %bitcast.3), channel_id=1, replica_groups=mesh['depth'=32,'rows'=16] {'depth','rows'}, dimensions={0} | all-to-all | bytes 1048576 | tf_op jit(solution)/shard_map/all_to_all | solution.py:487
  78.0 3.5 %rows.1 = f32[32,5,4,128]{3,2,1,0:T(4,128)S(1)} custom-call(s32[1024,128]{1,0:T(8,128)S(1)} %bitcast.2, f32[3,32,128]{2,1,0:T(8,128)S(1)} %get-tuple-element.11.par_ref, bf16[2,2,256,256]{3,2,1,0:T(8,128)(2,1)S(1)} %get-tuple-element.12.row_ref, f32[2,16,256]{2,1,0:T(8,128)S(1)} %get-tuple-element.13.twist_ref), custom_call_target="tpu_custom_call" | custom-call | flops 1000000000 | bytes 2200000 | tf_op jit(solution)/shard_map/rows/pallas_call | solution.py:491
  81.4 16.4 %all_to_all.16.in_ref = f32[32,5,4,128]{3,2,1,0:T(4,128)S(1)} all-to-all(f32[32,5,4,128]{3,2,1,0:T(4,128)S(1)} %rows.1), channel_id=1, replica_groups=mesh['depth'=32,'rows'=16] {'depth'}, dimensions={0} | all-to-all | bytes 655360 | tf_op jit(solution)/shard_map/all_to_all | solution.py:513
  97.8 0.7 merge.1
Async XLA Ops:
  4.7 33.3 %all-to-all-start = ((bf16[32,24,128]{2,1,0:T(8,128)(2,1)}), bf16[32,24,128]{2,1,0:T(8,128)(2,1)S(1)}, u32[]{:S(2)}, u32[]{:S(2)}) async-start(bf16[32,24,128]{2,1,0:T(8,128)(2,1)} %pick.1), calls=%async_computation | async-start | bytes 393216 | tf_op jit(solution)/shard_map/all_to_all | solution.py:438
  26.1 1.3 %copy-start = (bf16[8,2,256,256]{3,2,1,0:T(8,128)(2,1)}, bf16[8,2,256,256]{3,2,1,0:T(8,128)(2,1)S(1)}, u32[]{:S(2)}) copy-start(bf16[8,2,256,256]{3,2,1,0:T(8,128)(2,1)S(1)} %get-tuple-element.9.low_hbm) | copy-start | bytes 6291460

commit v5 on v4

--- a/solution.py
+++ b/solution.py
@@ -234,7 +234,7 @@
             acc[half] += parts[half] + parts[half + 2]
         return carry
 
-    lax.fori_loop(0, BLOCKS, step, 0, unroll=4)
+    lax.fori_loop(0, BLOCKS, step, 0, unroll=8)
     lane = lax.broadcasted_iota(jnp.int32, (8, 128), 1)
     group = (lane >> 2) & 3
     plane = z[0:8]

time: 99.3 us -> 98.7 us (level)
  no operation moved by 1% of the time
where the time goes in v5:
time: 98.7 us; the launch traced here: 98 us
  blocking collectives  49 us (50%)
  starting transfers between devices  19.2 us (19%)
  Pallas kernels  15.3 us (16%)
  waiting for transfers between devices  10.5 us (11%)
  between operations  2.62 us (3%)
  local copies, waits for them, and re-layouts  1.32 us (1%)
    all_to_all x1, blocking collectives, shards(): lax.all_to_all(messages.reshape(512, 1, 256), ALL, split_axis=0, concat_a...  32.6 us
    all_to_all x1, starting transfers between devices, shards(): lax.all_to_all(picked, ALL, split_axis=0, concat_axis=0, tiled=True, axis...  19.2 us
    all_to_all x1, blocking collectives, shards(): lax.all_to_all(records, 'depth', split_axis=0, concat_axis=0, tiled=True)  16.4 us
    all_to_all x1, waiting for transfers between devices, shards(): lax.all_to_all(picked, ALL, split_axis=0, concat_axis=0, tiled=True, axis...  10.5 us
    pallas_call x1, Pallas kernels, shards(): pl.pallas_call(column_kernel, in_specs=[whole((32, 24, 128)), whole((BLOC...  6.86 us
    pallas_call x1, Pallas kernels, shards(): pl.pallas_call(row_kernel, in_specs=[whole((1024, 128)), whole((3, 32, 12...  3.46 us
    pallas_call x1, Pallas kernels, shards(): pl.pallas_call(table_kernel, grid=(BLOCKS,), in_specs=[], out_specs=[pl.B...  2.18 us
    pallas_call x1, Pallas kernels, shards(): pl.pallas_call(pick_kernel, in_specs=[smem, smem, smem, pl.BlockSpec(memo...  2.13 us
  transfers between devices with their start and end apart: 1, of which 1 were waited for; matrix products, arithmetic and copies ran while one was open for 0% of the time, Pallas kernels for 2%

profile of v5, /device:TPU:1, one launch (start us, length us, event | category | flops | bytes accessed | tf_op | source)
XLA Modules:
  0.0 98.0 jit_solution(6596632717636426720)
XLA Ops:
  2.6 2.1 %pick.1 = bf16[32,24,128]{2,1,0:T(8,128)(2,1)} custom-call(s32[1]{0:T(128)S(6)} %copy.7.z_ref, s32[1]{0:T(128)S(6)} %copy.8.width_ref, f32[1]{0:T(128)S(6)} %copy.9.gain_ref, bf16[2,256,4096]{2,1,0:T(8,128)(2,1)} %spec_ref.1), custom_call_target="tpu_custom_call" | custom-call | flops 50000000 | bytes 300000 | tf_op jit(solution)/shard_map/pick/pallas_call | solution.py:427
  4.7 19.2 %all-to-all-start = ((bf16[32,24,128]{2,1,0:T(8,128)(2,1)}), bf16[32,24,128]{2,1,0:T(8,128)(2,1)S(1)}, u32[]{:S(2)}, u32[]{:S(2)}) async-start(bf16[32,24,128]{2,1,0:T(8,128)(2,1)} %pick.1), calls=%async_computation | async-start | bytes 393216 | tf_op jit(solution)/shard_map/all_to_all | solution.py:438
  24.0 2.2 %tables.1 = (bf16[8,2,256,256]{3,2,1,0:T(8,128)(2,1)S(1)}, bf16[8,2,256,256]{3,2,1,0:T(8,128)(2,1)S(1)}, bf16[2,2,256,256]{3,2,1,0:T(8,128)(2,1)S(1)}, f32[2,16,256]{2,1,0:T(8,128)S(1)}) custom-call(), custom_call_target="tpu_custom_call" | custom-call | flops 30000000 | bytes 5000000 | tf_op jit(solution)/shard_map/tables/pallas_call | solution.py:442
  26.1 0.0 copy-start
  26.2 1.3 %copy-done = bf16[8,2,256,256]{3,2,1,0:T(8,128)(2,1)} copy-done((bf16[8,2,256,256]{3,2,1,0:T(8,128)(2,1)}, bf16[8,2,256,256]{3,2,1,0:T(8,128)(2,1)S(1)}, u32[]{:S(2)}) %copy-start) | copy-done | bytes 2097176
  27.5 10.5 %all-to-all-done.spec_ref = bf16[32,24,128]{2,1,0:T(8,128)(2,1)S(1)} async-done(((bf16[32,24,128]{2,1,0:T(8,128)(2,1)}), bf16[32,24,128]{2,1,0:T(8,128)(2,1)S(1)}, u32[]{:S(2)}, u32[]{:S(2)}) %all-to-all-start) | async-done | bytes 196640 | tf_op jit(solution)/shard_map/all_to_all | solution.py:438
  38.0 6.9 %columns.1 = (s32[1024,128]{1,0:T(8,128)S(1)}, f32[3,32,128]{2,1,0:T(8,128)S(1)}) custom-call(bf16[32,24,128]{2,1,0:T(8,128)(2,1)S(1)} %all-to-all-done.spec_ref, bf16[8,2,256,256]{3,2,1,0:T(8,128)(2,1)S(1)} %get-tuple-element.8.high_ref, bf16[8,2,256,256]{3,2,1,0:T(8,128)(2,1)} %copy-done), custom_call_target="tpu_custom_call" | custom-call | flops 6499999744 | bytes 8000000 | tf_op jit(solution)/shard_map/columns/pallas_call | solution.py:464
  44.8 32.6 %all_to_all.15 = s32[512,1,256]{2,1,0:T(1,128)S(1)} all-to-all(s32[512,1,256]{2,1,0:T(1,128)S(1)} %bitcast.3), channel_id=1, replica_groups=mesh['depth'=32,'rows'=16] {'depth','rows'}, dimensions={0} | all-to-all | bytes 1048576 | tf_op jit(solution)/shard_map/all_to_all | solution.py:487
  77.5 3.5 %rows.1 = f32[32,5,4,128]{3,2,1,0:T(4,128)S(1)} custom-call(s32[1024,128]{1,0:T(8,128)S(1)} %bitcast.2, f32[3,32,128]{2,1,0:T(8,128)S(1)} %get-tuple-element.11.par_ref, bf16[2,2,256,256]{3,2,1,0:T(8,128)(2,1)S(1)} %get-tuple-element.12.row_ref, f32[2,16,256]{2,1,0:T(8,128)S(1)} %get-tuple-element.13.twist_ref), custom_call_target="tpu_custom_call" | custom-call | flops 1000000000 | bytes 2200000 | tf_op jit(solution)/shard_map/rows/pallas_call | solution.py:491
  80.9 16.4 %all_to_all.16.in_ref = f32[32,5,4,128]{3,2,1,0:T(4,128)S(1)} all-to-all(f32[32,5,4,128]{3,2,1,0:T(4,128)S(1)} %rows.1), channel_id=1, replica_groups=mesh['depth'=32,'rows'=16] {'depth'}, dimensions={0} | all-to-all | bytes 655360 | tf_op jit(solution)/shard_map/all_to_all | solution.py:513
  97.3 0.7 merge.1
Async XLA Ops:
  4.7 33.3 %all-to-all-start = ((bf16[32,24,128]{2,1,0:T(8,128)(2,1)}), bf16[32,24,128]{2,1,0:T(8,128)(2,1)S(1)}, u32[]{:S(2)}, u32[]{:S(2)}) async-start(bf16[32,24,128]{2,1,0:T(8,128)(2,1)} %pick.1), calls=%async_computation | async-start | bytes 393216 | tf_op jit(solution)/shard_map/all_to_all | solution.py:438
  26.1 1.3 %copy-start = (bf16[8,2,256,256]{3,2,1,0:T(8,128)(2,1)}, bf16[8,2,256,256]{3,2,1,0:T(8,128)(2,1)S(1)}, u32[]{:S(2)}) copy-start(bf16[8,2,256,256]{3,2,1,0:T(8,128)(2,1)S(1)} %get-tuple-element.9.low_hbm) | copy-start | bytes 6291460
